TPU v7x, 32 devices: a whole 2x2x4 slice. The times are simulated.
32 devices in a mesh: lat: 4 (over x, core), lon: 8 (over z, y).
Axes of the slice: x: 2, y: 2, z: 4, core: 2. Of those that a mesh axis runs over, the one named last changes fastest.
Arguments:
- fine_tokens: bfloat16 [2, 48, 96, 512], P(None, 'lat', 'lon'), may hold values from -6 to 6
- qkv_weight: bfloat16 [512, 1536], P(None, 'lat'), may hold values from -2 to 2
- proj_weight: bfloat16 [512, 512], P(None, 'lat'), may hold values from -0.25 to 0.25
- merge_one: bfloat16 [2048, 1024], P(None, 'lat'), may hold values from -0.125 to 0.125
- merge_two: bfloat16 [4096, 2048], P('lon'), may hold values from -0.09375 to 0.09375
- mlp_in: bfloat16 [2048, 8192], P(None, 'lon'), may hold values from -0.125 to 0.125
- mlp_out: bfloat16 [8192, 2048], P('lon'), may hold values from -0.125 to 0.125
- split_weight: bfloat16 [2048, 4096], P(None, 'lon'), may hold values from -0.125 to 0.125
Outputs:
- fine_out: float32 [2, 48, 96, 512], P(None, 'lat', 'lon')
- mid_out: float32 [2, 24, 48, 1024], P(None, 'lat', 'lon')
All inputs are finite; a program needn't handle non-finite values.
Results may differ from a plain program's by a relative error of at most 0.029.
Values may be sent and summed in bfloat16 or wider, within the bound.
A program may use at most 64 MiB of HBM per device.

v0:
```python
import math

import jax
import jax.numpy as jnp
from jax import lax
from jax.sharding import PartitionSpec as P

MID = 1024
HEADS = 8
WIN_R = 6
WIN_C = 12
SHIFT_R = 3
SHIFT_C = 6


def from_behind(value, axis, steps):
    count = lax.axis_size(axis)
    pairs = [(source, (source + steps) % count) for source in range(count)]
    return lax.ppermute(value, axis, pairs)


def layer_norm(values):
    centre = jnp.mean(values, axis=-1, keepdims=True)
    shifted = values - centre
    spread = jnp.mean(shifted * shifted, axis=-1, keepdims=True)
    return shifted * lax.rsqrt(spread + 1e-05)


def cat_four(grid):
    lev, rows, cols, width = grid.shape
    grid = grid.reshape(lev, rows // 2, 2, cols // 2, 2, width).transpose(0, 1, 3, 2, 4, 5)
    return grid.reshape(lev * (rows // 2) * (cols // 2), 4 * width)


def on_device(
    fine_tokens, qkv_weight, proj_weight, merge_one, merge_two, mlp_in, mlp_out, split_weight
):
    levels, rows, cols, width = fine_tokens.shape
    lat_count = lax.axis_size("lat")
    head_dim = width // HEADS
    full_qkv, full_proj = (
        lax.all_gather(qkv_weight, "lat", axis=1, tiled=True),
        lax.all_gather(proj_weight, "lat", axis=1, tiled=True),
    )
    came = from_behind(fine_tokens[:, :, :SHIFT_C], "lon", -1)
    col_moved = jnp.concatenate([fine_tokens[:, :, SHIFT_C:], came], axis=2)
    came = from_behind(col_moved[:, :SHIFT_R], "lat", -1)
    moved = jnp.concatenate([col_moved[:, SHIFT_R:], came], axis=1)
    normed = layer_norm(moved.astype(jnp.float32)).astype(jnp.bfloat16).reshape(-1, width)
    qkv = jnp.dot(normed, full_qkv, preferred_element_type=jnp.float32).astype(jnp.bfloat16)
    row_wins = rows // WIN_R
    col_wins = cols // WIN_C
    wins = row_wins * col_wins
    tokens = levels * WIN_R * WIN_C
    parts = qkv.reshape(levels, row_wins, WIN_R, col_wins, WIN_C, 3, HEADS, head_dim)
    parts = parts.transpose(1, 3, 0, 2, 4, 5, 6, 7).reshape(wins, tokens, 3, HEADS, head_dim)
    scores = jnp.einsum(
        "wqhd,wkhd->whqk", parts[:, :, 0], parts[:, :, 1], preferred_element_type=jnp.float32
    )
    scores = scores / math.sqrt(head_dim)
    global_rows = lax.axis_index("lat") * rows + jnp.arange(rows, dtype=jnp.int32)
    wrapped = (global_rows >= rows * lat_count - SHIFT_R).astype(jnp.int32).reshape(row_wins, WIN_R)
    labels = jnp.broadcast_to(
        wrapped[:, None, None, :, None], (row_wins, col_wins, levels, WIN_R, WIN_C)
    )
    labels = labels.reshape(wins, tokens)
    allowed = labels[:, :, None] == labels[:, None, :]
    scores = jnp.where(allowed[:, None], scores, jnp.float32(-1000000000.0))
    top = jnp.max(scores, axis=-1, keepdims=True)
    expo = jnp.exp(scores - top)
    probs = (expo / jnp.sum(expo, axis=-1, keepdims=True)).astype(jnp.bfloat16)
    heads_out = jnp.einsum(
        "whqk,wkhd->wqhd", probs, parts[:, :, 2], preferred_element_type=jnp.float32
    )
    heads_out = heads_out.astype(jnp.bfloat16).reshape(
        row_wins, col_wins, levels, WIN_R, WIN_C, width
    )
    heads_out = heads_out.transpose(2, 0, 3, 1, 4, 5).reshape(-1, width)
    attn = jnp.dot(heads_out, full_proj, preferred_element_type=jnp.float32).astype(jnp.bfloat16)
    attn = attn.reshape(levels, rows, cols, width)
    came = from_behind(attn[:, rows - SHIFT_R :], "lat", 1)
    row_back = jnp.concatenate([came, attn[:, : rows - SHIFT_R]], axis=1)
    came = from_behind(row_back[:, :, cols - SHIFT_C :], "lon", 1)
    back = jnp.concatenate([came, row_back[:, :, : cols - SHIFT_C]], axis=2)
    fine_out = fine_tokens.astype(jnp.float32) + back.astype(jnp.float32)
    normed1 = layer_norm(cat_four(fine_out)).astype(jnp.bfloat16)
    merged1 = jnp.dot(
        normed1,
        lax.all_gather(merge_one, "lat", axis=1, tiled=True),
        preferred_element_type=jnp.float32,
    ).astype(jnp.bfloat16)
    merged1 = merged1.reshape(levels, rows // 2, cols // 2, MID)
    normed2 = layer_norm(cat_four(merged1.astype(jnp.float32))).astype(jnp.bfloat16)
    own_count = normed2.shape[0]
    feature_parts = lax.all_to_all(normed2, "lon", split_axis=1, concat_axis=0, tiled=True)
    partial_value = jnp.dot(feature_parts, merge_two, preferred_element_type=jnp.float32)
    merged2 = lax.psum(partial_value.astype(jnp.bfloat16), "lon").astype(jnp.float32)
    normed3 = layer_norm(merged2).astype(jnp.bfloat16)
    act = jax.nn.gelu(jnp.dot(normed3, mlp_in, preferred_element_type=jnp.float32)).astype(
        jnp.bfloat16
    )
    mlp_own = lax.psum_scatter(
        jnp.dot(act, mlp_out, preferred_element_type=jnp.float32).astype(jnp.bfloat16),
        "lon",
        scatter_dimension=0,
        tiled=True,
    ).astype(jnp.float32)
    own_merged = lax.dynamic_slice_in_dim(merged2, lax.axis_index("lon") * own_count, own_count, 0)
    coarse = (own_merged + mlp_own).astype(jnp.bfloat16)
    split_cols = jnp.dot(
        lax.all_gather(coarse, "lon", axis=0, tiled=True),
        split_weight,
        preferred_element_type=jnp.float32,
    ).astype(jnp.bfloat16)
    pieces = lax.all_to_all(split_cols, "lon", split_axis=0, concat_axis=1, tiled=True)
    pieces = pieces.reshape(levels, rows // 4, cols // 4, 2, 2, MID).transpose(0, 1, 3, 2, 4, 5)
    pieces = pieces.reshape(levels, rows // 2, cols // 2, MID)
    mid_out = merged1.astype(jnp.float32) + pieces.astype(jnp.float32)
    return (fine_out, mid_out)


def solution(mesh):
    return jax.shard_map(
        on_device,
        mesh=mesh,
        in_specs=(
            P(None, "lat", "lon", None),
            P(None, "lat"),
            P(None, "lat"),
            P(None, "lat"),
            P("lon", None),
            P(None, "lon"),
            P("lon", None),
            P(None, "lon"),
        ),
        out_specs=(P(None, "lat", "lon", None), P(None, "lat", "lon", None)),
        check_vma=False,
    )
```

profile of v0, /device:TPU:0, one launch (start us, length us, event | category | flops | bytes accessed | tf_op | source)
XLA Modules:
  0.0 264.7 jit_solution(7980321667929942150)
XLA Ops:
  7.2 0.7 all-gather.4.cloned.1.call-update
  8.0 0.7 all-gather.6.cloned.1.call-update
  8.7 1.2 fusion.58
  9.9 6.1 %collective-permute-start = (bf16[2,12,6,512]{3,0,2,1:T(2,128)(2,1)S(1)}, bf16[2,12,6,512]{3,0,2,1:T(2,128)(2,1)S(1)}, u32[]{:S(2)}, u32[]{:S(2)}) collective-permute-start(bf16[2,12,6,512]{3,0,2,1:T(2,128)(2,1)S(1)} %get-tuple-element.14), channel_id=1, source_target_pairs={{0,7},{1,0},{2,1},{3,2},{4,3},{5,4},{6,5},{7,6},{8,15},{9,8},{10,9... | collective-permute-start | bytes 442376 | tf_op jit(solution)/shard_map/ppermute | solution.py:19
  16.3 8.8 %all_gather.13 = bf16[512,512]{1,0:T(8,128)(2,1)} all-gather(bf16[512,128]{1,0:T(8,128)(2,1)S(1)} %copy-done.5), channel_id=1, replica_groups=mesh['lat'=4,'lon'=8] {'lat'}, dimensions={1}, use_global_device_ids=true | all-gather | bytes 655360 | tf_op jit(solution)/shard_map/all_gather | solution.py:43
  25.2 1.9 collective-permute-start.1
  27.4 2.8 %collective-permute-done.1 = bf16[2,3,12,512]{3,0,2,1:T(2,128)(2,1)S(1)} collective-permute-done((bf16[2,3,12,512]{3,0,2,1:T(2,128)(2,1)S(1)}, bf16[2,3,12,512]{3,0,2,1:T(2,128)(2,1)S(1)}, u32[]{:S(2)}, u32[]{:S(2)}) %collective-permute-start.1) | collective-permute-done | bytes 73760 | tf_op jit(solution)/shard_map/ppermute | solution.py:19
  30.8 0.6 multiply_reduce_fusion.2
  32.3 0.9 reshape.193
  33.3 2.3 convolution_convert_fusion
  35.6 2.0 reshape.185
  37.6 1.8 copy.82
  39.4 1.1 fusion.57
  40.5 2.3 copy.102
  42.8 1.2 copy.103
  44.4 3.7 %fusion.59 = (f32[2,8,144]{2,1,0:T(8,128)S(1)}, f32[2,8,144,144]{2,3,1,0:T(8,128)}) fusion(pred[2,144,144]{1,2,0:T(8,128)(4,1)S(1)} %broadcast_compare_fusion, bf16[2,144,1,8,64]{1,4,3,0,2:T(8,128)(2,1)} %copy.103, bf16[2,144,1,8,64]{1,4,3,0,2:T(8,128)(2,1)} %copy.102), kind=kOutput, calls=%fused_computation.86 | convolution fusion | flops 43794576 | bytes 1967616 | tf_op jit(solution)/shard_map/sub | solution.py:70
  48.0 2.8 %fusion.3 = bf16[2,144,8,64]{1,3,2,0:T(8,128)(2,1)} fusion(f32[2,8,144,144]{2,3,1,0:T(8,128)} %get-tuple-element.16, f32[2,8,144]{2,1,0:T(8,128)S(1)} %get-tuple-element.15, bf16[2,144,1,8,64]{1,4,3,0,2:T(8,128)(2,1)S(1)} %copy.101), kind=kOutput, calls=%fused_computation.9 | convolution fusion | flops 43278336 | bytes 1926144 | tf_op jit(solution)/shard_map/whqk,wkhd->wqhd/dot_general | solution.py:72
  50.8 1.6 copy.87
  52.8 0.8 reshape.188
  53.6 2.0 convolution_convert_fusion.4
  55.6 1.0 reshape.189
  56.6 1.2 collective-permute-start.2
  57.8 5.4 %collective-permute-done.2 = bf16[2,3,12,512]{3,2,1,0:T(8,128)(2,1)S(1)} collective-permute-done((bf16[2,3,12,512]{3,2,1,0:T(8,128)(2,1)S(1)}, bf16[2,3,12,512]{3,2,1,0:T(8,128)(2,1)S(1)}, u32[]{:S(2)}, u32[]{:S(2)}) %collective-permute-start.2) | collective-permute-done | bytes 73760 | tf_op jit(solution)/shard_map/ppermute | solution.py:19
  63.3 0.9 collective-permute-start.3
  64.2 7.7 %collective-permute-done.3 = bf16[2,12,6,512]{3,2,1,0:T(8,128)(2,1)S(1)} collective-permute-done((bf16[2,12,6,512]{3,2,1,0:T(8,128)(2,1)S(1)}, bf16[2,12,6,512]{3,2,1,0:T(8,128)(2,1)S(1)}, u32[]{:S(2)}, u32[]{:S(2)}) %collective-permute-start.3) | collective-permute-done | bytes 147488 | tf_op jit(solution)/shard_map/ppermute | solution.py:19
  72.1 0.5 copy.98
  72.6 1.1 copy.90
  74.7 2.4 reshape.191
  77.3 3.3 %fusion.7 = f32[72,1024]{1,0:T(8,128)S(1)} fusion(bf16[2048,1024]{1,0:T(8,128)(2,1)} %all-gather.6.cloned.1.call-done, f32[72,2048]{1,0:T(8,128)} %reshape.191, f32[72]{0:T(128)S(1)} %rsqrt.44, f32[72]{0:T(128)S(1)} %div.52), kind=kOutput, calls=%fused_computation.18 | convolution fusion | flops 302579712 | bytes 5079616 | tf_op jit(solution)/shard_map/dot_general | solution.py:87
  81.9 10.2 %all_to_all.29 = bf16[18,8,512]{2,0,1:T(8,128)(2,1)S(1)} all-to-all(bf16[18,8,512]{2,0,1:T(8,128)(2,1)S(1)} %copy.94), channel_id=1, replica_groups=mesh['lat'=4,'lon'=8] {'lon'}, dimensions={1} | all-to-all | bytes 294912 | tf_op jit(solution)/shard_map/all_to_all | solution.py:95
  92.1 1.3 convolution_convert_fusion.2
  93.4 70.7 %all-reduce.4.cloned.1.call-done = bf16[144,2048]{1,0:T(8,128)(2,1)} async-done(((bf16[144,2048]{1,0:T(8,128)(2,1)}), bf16[144,2048]{1,0:T(8,128)(2,1)}) %all-reduce.4.cloned.1.call-update) | async-done | bytes 589840 | tf_op jit(solution)/shard_map/psum | solution.py:97
  164.2 1.2 convert_reduce_fusion
  165.4 1.4 multiply_reduce_fusion
  166.8 6.1 %convolution_convert_fusion.1 = bf16[144,2048]{1,0:T(8,128)(2,1)} fusion(bf16[1024,2048]{1,0:T(8,128)(2,1)} %param.14, bf16[2048,1024]{1,0:T(8,128)(2,1)} %param.13, bf16[144,2048]{1,0:T(8,128)(2,1)} %all-reduce.4.cloned.1.call-done, f32[144]{0:T(256)S(1)} %add_rsqrt_fusion.3, f32[144]{0:T(256)S(1)} %broadcast_multiply_fusion.3), kind=kOutput, calls=%fused_computation.2 | convolution fusion | flops 1210761216 | bytes 9569408 | tf_op jit(solution)/shard_map/dot_general | solution.py:103
  172.9 26.7 %fusion = bf16[24,2048]{1,0:T(8,128)(2,1)S(1)} fusion(bf16[144,2048]{1,0:T(8,128)(2,1)} %convolution_convert_fusion.1), kind=kCustom, calls=%all-reduce-scatter | all-reduce-scatter fusion | flops 393217 | bytes 688640
  199.6 2.0 collective-permute-start.4
  201.7 2.5 collective-permute-start.5
  204.3 0.6 dynamic-slice.4
  205.5 1.1 convert_element_type.120
  207.3 1.0 fusion.44
  208.3 33.0 %all-gather = bf16[8,18,2048]{2,1,0:T(8,128)(2,1)S(1)} all-gather(bf16[1,18,2048]{2,1,0:T(8,128)(2,1)S(1)} %fusion.44), channel_id=1, replica_groups=mesh['lat'=4,'lon'=8] {'lon'}, dimensions={0}, use_global_device_ids=true | all-gather | bytes 663552 | tf_op jit(solution)/shard_map/all_gather | solution.py:111
  241.3 1.0 reshape.199
  242.3 2.3 convolution_convert_fusion.5
  244.5 0.7 all_to_all.25
  245.3 3.4 %all-to-all-start.1 = ((bf16[8,18,512]{2,1,0:T(8,128)(2,1)}), bf16[8,18,512]{2,1,0:T(8,128)(2,1)S(1)}, u32[]{:S(2)}, u32[]{:S(2)}) async-start(bf16[8,18,512]{2,1,0:T(8,128)(2,1)} %all_to_all.25), calls=%async_computation.1 | async-start | bytes 393216 | tf_op jit(solution)/shard_map/all_to_all | solution.py:115
  248.7 7.7 %all-to-all-done.1 = bf16[8,18,512]{2,1,0:T(8,128)(2,1)S(1)} async-done(((bf16[8,18,512]{2,1,0:T(8,128)(2,1)}), bf16[8,18,512]{2,1,0:T(8,128)(2,1)S(1)}, u32[]{:S(2)}, u32[]{:S(2)}) %all-to-all-start.1) | async-done | bytes 147488 | tf_op jit(solution)/shard_map/all_to_all | solution.py:115
  257.2 0.9 copy.99
  (75 shorter events, 7.4 us)
Async XLA Ops:
  7.2 84.9 %copy-start = (bf16[512,2048]{1,0:T(8,128)(2,1)S(1)}, bf16[512,2048]{1,0:T(8,128)(2,1)}, u32[]{:S(2)}) copy-start(bf16[512,2048]{1,0:T(8,128)(2,1)} %param.12) | copy-start | bytes 6291460
  7.2 9.1 %copy-start.5 = (bf16[512,128]{1,0:T(8,128)(2,1)S(1)}, bf16[512,128]{1,0:T(8,128)(2,1)}, u32[]{:S(2)}) copy-start(bf16[512,128]{1,0:T(8,128)(2,1)} %param.10) | copy-start | bytes 393220
  7.2 26.2 %all-gather.4.cloned.1.call-start = ((), (), s32[]{:S(2)}) async-start(), calls=%async_computation.2 | async-start | bytes 1966080 | tf_op jit(solution)/shard_map/all_gather | solution.py:42
  7.9 69.3 %all-gather.6.cloned.1.call-start = ((), (), s32[]{:S(2)}) async-start(), calls=%async_computation.3 | async-start | bytes 5242880 | tf_op jit(solution)/shard_map/all_gather | solution.py:89
  8.7 155.5 %all-reduce.4.cloned.1.call-start = ((), (), s32[]{:S(2)}) async-start(), calls=%async_computation.4 | async-start | bytes 1179648 | tf_op jit(solution)/shard_map/psum | solution.py:97
  9.9 15.2 %collective-permute-start = (bf16[2,12,6,512]{3,0,2,1:T(2,128)(2,1)S(1)}, bf16[2,12,6,512]{3,0,2,1:T(2,128)(2,1)S(1)}, u32[]{:S(2)}, u32[]{:S(2)}) collective-permute-start(bf16[2,12,6,512]{3,0,2,1:T(2,128)(2,1)S(1)} %get-tuple-element.14), channel_id=1, source_target_pairs={{0,7},{1,0},{2,1},{3,2},{4,3},{5,4},{6,5},{7,6},{8,15},{9,8},{10,9... | collective-permute-start | bytes 442376 | tf_op jit(solution)/shard_map/ppermute | solution.py:19
  25.2 5.0 %collective-permute-start.1 = (bf16[2,3,12,512]{3,0,2,1:T(2,128)(2,1)S(1)}, bf16[2,3,12,512]{3,0,2,1:T(2,128)(2,1)S(1)}, u32[]{:S(2)}, u32[]{:S(2)}) collective-permute-start(bf16[2,3,12,512]{3,0,2,1:T(2,128)(2,1)S(1)} %pad_maximum_fusion.1), channel_id=1, source_target_pairs={{0,24},{8,0},{16,8},{24,16},{1,25},{9,1},{17,9},{25,17},{2,26},{10... | collective-permute-start | bytes 221192 | tf_op jit(solution)/shard_map/ppermute | solution.py:19
  50.8 2.8 %copy-start.3 = (bf16[512,512]{1,0:T(8,128)(2,1)S(1)}, bf16[512,512]{1,0:T(8,128)(2,1)}, u32[]{:S(2)}) copy-start(bf16[512,512]{1,0:T(8,128)(2,1)} %all_gather.13) | copy-start | bytes 1572868
  52.8 19.1 %copy-start.4 = (bf16[2,12,12,512]{3,0,2,1:T(2,128)(2,1)S(1)}, bf16[2,12,12,512]{3,0,2,1:T(2,128)(2,1)}, u32[]{:S(2)}) copy-start(bf16[2,12,12,512]{3,0,2,1:T(2,128)(2,1)} %param.8) | copy-start | bytes 884740
  56.6 6.6 %collective-permute-start.2 = (bf16[2,3,12,512]{3,2,1,0:T(8,128)(2,1)S(1)}, bf16[2,3,12,512]{3,2,1,0:T(8,128)(2,1)S(1)}, u32[]{:S(2)}, u32[]{:S(2)}) collective-permute-start(bf16[2,3,12,512]{3,2,1,0:T(8,128)(2,1)S(1)} %slice.49), channel_id=1, source_target_pairs={{0,8},{8,16},{16,24},{24,0},{1,9},{9,17},{17,25},{25,1},{2,10},{10... | collective-permute-start | bytes 221192 | tf_op jit(solution)/shard_map/ppermute | solution.py:19
  63.3 8.6 %collective-permute-start.3 = (bf16[2,12,6,512]{3,2,1,0:T(8,128)(2,1)S(1)}, bf16[2,12,6,512]{3,2,1,0:T(8,128)(2,1)S(1)}, u32[]{:S(2)}, u32[]{:S(2)}) collective-permute-start(bf16[2,12,6,512]{3,2,1,0:T(8,128)(2,1)S(1)} %fusion.35), channel_id=1, source_target_pairs={{0,1},{1,2},{2,3},{3,4},{4,5},{5,6},{6,7},{7,0},{8,9},{9,10},{10,1... | collective-permute-start | bytes 442376 | tf_op jit(solution)/shard_map/ppermute | solution.py:19
  72.5 8.0 %copy-start.1 = (f32[2,12,12,512]{3,0,2,1:T(2,128)}, f32[2,12,12,512]{3,0,2,1:T(2,128)S(1)}, u32[]{:S(2)}) copy-start(f32[2,12,12,512]{3,0,2,1:T(2,128)S(1)} %copy.98) | copy-start | bytes 1769476
  166.8 37.5 %copy-start.6 = (u32[32]{0:T(128)S(1)}, u32[32]{0:T(128)}, u32[]{:S(2)}) copy-start(u32[32]{0:T(128)} %constant.64) | copy-start | bytes 388
  166.8 38.7 %copy-start.2 = (bf16[144,2048]{1,0:T(8,128)(2,1)S(1)}, bf16[144,2048]{1,0:T(8,128)(2,1)}, u32[]{:S(2)}) copy-start(bf16[144,2048]{1,0:T(8,128)(2,1)} %all-reduce.4.cloned.1.call-done) | copy-start | bytes 1769476
  199.6 7.2 %collective-permute-start.4 = (bf16[24,2048]{1,0:T(8,128)(2,1)S(1)}, bf16[24,2048]{1,0:T(8,128)(2,1)S(1)}, u32[]{:S(2)}, u32[]{:S(2)}) collective-permute-start(bf16[24,2048]{1,0:T(8,128)(2,1)S(1)} %fusion), channel_id=1, source_target_pairs={{0,1},{1,2},{2,3},{3,4},{4,5},{5,6},{6,7},{8,9},{9,10},{10,11},{11... | collective-permute-start | bytes 294920
  201.7 5.1 %collective-permute-start.5 = (bf16[18,2048]{1,0:T(8,128)(2,1)S(1)}, bf16[18,2048]{1,0:T(8,128)(2,1)S(1)}, u32[]{:S(2)}, u32[]{:S(2)}) collective-permute-start(bf16[18,2048]{1,0:T(8,128)(2,1)S(1)} %slice.53), channel_id=1, source_target_pairs={{0,2},{1,3},{2,4},{3,5},{4,6},{5,7},{8,10},{9,11},{10,12},{11,13},... | collective-permute-start | bytes 221192
  245.3 11.1 %all-to-all-start.1 = ((bf16[8,18,512]{2,1,0:T(8,128)(2,1)}), bf16[8,18,512]{2,1,0:T(8,128)(2,1)S(1)}, u32[]{:S(2)}, u32[]{:S(2)}) async-start(bf16[8,18,512]{2,1,0:T(8,128)(2,1)} %all_to_all.25), calls=%async_computation.1 | async-start | bytes 393216 | tf_op jit(solution)/shard_map/all_to_all | solution.py:115
Sparse Core Ops, SparseCore 0:
  9.6 23.7 all-gather.3
  34.9 35.4 all-gather.5
  93.5 70.5 all-reduce.3
where the time goes:
time: 266 us; the launch traced here: 265 us
  waiting for transfers between devices  96.2 us (36%)
  blocking collectives  78.7 us (30%)
  local copies, waits for them, and re-layouts  24.9 us (9%)
  matrix products  23.6 us (9%)
  starting transfers between devices  18 us (7%)
  between operations  14.8 us (6%)
  other arithmetic  8.32 us (3%)
    psum x1, waiting for transfers between devices, on_device(): lax.psum(partial_value.astype(jnp.bfloat16), 'lon').astype(jnp.float32)  70.7 us
    all_gather x1, blocking collectives, on_device(): lax.all_gather(coarse, 'lon', axis=0, tiled=True)  33 us
    unnamed x1, blocking collectives  26.7 us
    ppermute x4, waiting for transfers between devices, from_behind(): return lax.ppermute(value, axis, pairs)  16 us
    all_to_all x1, blocking collectives, on_device(): lax.all_to_all(normed2, 'lon', split_axis=1, concat_axis=0, tiled=True)  10.2 us
    ppermute x4, starting transfers between devices, from_behind(): return lax.ppermute(value, axis, pairs)  9.96 us
    all_gather x1, blocking collectives, on_device(): lax.all_gather(proj_weight, 'lat', axis=1, tiled=True)  8.79 us
    all_to_all x1, waiting for transfers between devices, on_device(): lax.all_to_all(split_cols, 'lon', split_axis=0, concat_axis=1, tiled=True)  7.67 us
  transfers between devices with their start and end apart: 10, of which 7 were waited for; matrix products, arithmetic and copies ran while one was open for 13% of the time, Pallas kernels for 0%

commit v1 on v0

--- a/solution.py
+++ b/solution.py
@@ -3,6 +3,8 @@
 import jax
 import jax.numpy as jnp
 from jax import lax
+from jax.experimental import pallas as pl
+from jax.experimental.pallas import tpu as pltpu
 from jax.sharding import PartitionSpec as P
 
 MID = 1024
@@ -30,6 +32,232 @@
     lev, rows, cols, width = grid.shape
     grid = grid.reshape(lev, rows // 2, 2, cols // 2, 2, width).transpose(0, 1, 3, 2, 4, 5)
     return grid.reshape(lev * (rows // 2) * (cols // 2), 4 * width)
+
+
+def coarse_kernel(
+    blocks_ref, two_hbm, in_hbm, out_hbm, split_hbm, pieces_ref,
+    two, w_in, w_out, split, landed, features, sent, summed, own, gathered, normed, act,
+    sent2, summed2, gathered2, cols, sent3, landed3,
+    load_sem, send_sem, recv_sem,
+):
+    count = lax.axis_size("lon")
+    me = lax.axis_index("lon")
+    own_count = blocks_ref.shape[1]
+    width = own.shape[1]
+    loads = [
+        pltpu.make_async_copy(source, target, load_sem.at[index])
+        for index, (source, target) in enumerate(
+            ((two_hbm, two), (in_hbm, w_in), (out_hbm, w_out), (split_hbm, split))
+        )
+    ]
+    for load in loads:
+        load.start()
+    barrier = pltpu.get_barrier_semaphore()
+
+    def greet(step, carry):
+        peer = lax.rem(me + step, count)
+        pl.semaphore_signal(
+            barrier, inc=1, device_id={"lon": peer}, device_id_type=pl.DeviceIdType.MESH
+        )
+        return carry
+
+    lax.fori_loop(1, count, greet, 0)
+    pl.semaphore_wait(barrier, count - 1)
+
+    def copy_to(phase, peer, source, target):
+        return pltpu.make_async_remote_copy(
+            src_ref=source,
+            dst_ref=target.at[me],
+            send_sem=send_sem.at[phase, peer],
+            recv_sem=recv_sem.at[phase, me],
+            device_id={"lon": peer},
+            device_id_type=pl.DeviceIdType.MESH,
+        )
+
+    def wait_from(phase, target):
+        def body(step, carry):
+            peer = lax.rem(me + step, count)
+            pltpu.make_async_remote_copy(
+                src_ref=target.at[peer],
+                dst_ref=target.at[peer],
+                send_sem=send_sem.at[phase, peer],
+                recv_sem=recv_sem.at[phase, peer],
+                device_id={"lon": peer},
+                device_id_type=pl.DeviceIdType.MESH,
+            ).wait_recv()
+            return carry
+
+        lax.fori_loop(1, count, body, 0)
+
+    def wait_sent(phase, source_of, target):
+        def body(step, carry):
+            peer = lax.rem(me + step, count)
+            copy_to(phase, peer, source_of(peer), target).wait_send()
+            return carry
+
+        lax.fori_loop(1, count, body, 0)
+
+    def scatter_products(phase, left, weight, send, target):
+        def product(peer):
+            cut = pl.ds(pl.multiple_of(peer * width, width), width)
+            return jnp.dot(left[...], weight[:, cut], preferred_element_type=jnp.float32)
+
+        def body(step, carry):
+            peer = lax.rem(me + step, count)
+            send[peer] = product(peer).astype(jnp.bfloat16)
+            copy_to(phase, peer, send.at[peer], target).start()
+            return carry
+
+        lax.fori_loop(1, count, body, 0)
+        total = product(me)
+        wait_from(phase, target)
+
+        def add(step, total):
+            return total + target[lax.rem(me + step, count)].astype(jnp.float32)
+
+        return lax.fori_loop(1, count, add, total)
+
+    def gather(phase, target):
+        def body(step, carry):
+            copy_to(phase, lax.rem(me + step, count), target.at[me], target).start()
+            return carry
+
+        lax.fori_loop(1, count, body, 0)
+        wait_from(phase, target)
+
+    def first(step, carry):
+        peer = lax.rem(me + step, count)
+        copy_to(0, peer, blocks_ref.at[peer], landed).start()
+        return carry
+
+    lax.fori_loop(1, count, first, 0)
+    landed[me] = blocks_ref[me]
+    wait_from(0, landed)
+    for index in range(count):
+        features[index * own_count : (index + 1) * own_count] = landed[index].astype(jnp.float32)
+    normed[:, : features.shape[1]] = features[...].astype(jnp.bfloat16)
+    loads[0].wait()
+    merged = scatter_products(1, normed.at[:, : features.shape[1]], two, sent, summed)
+    own[...] = merged
+    gathered[me] = merged.astype(jnp.bfloat16)
+    gather(2, gathered)
+
+    total_width = count * width
+    centre = gathered[0].astype(jnp.float32).sum(axis=-1, keepdims=True)
+    for index in range(1, count):
+        centre += gathered[index].astype(jnp.float32).sum(axis=-1, keepdims=True)
+    centre = centre / total_width
+    spread = jnp.zeros_like(centre)
+    for index in range(count):
+        shifted = gathered[index].astype(jnp.float32) - centre
+        spread += (shifted * shifted).sum(axis=-1, keepdims=True)
+    scale = lax.rsqrt(spread / total_width + 1e-05)
+    for index in range(count):
+        shifted = gathered[index].astype(jnp.float32) - centre
+        normed[:, index * width : (index + 1) * width] = (shifted * scale).astype(jnp.bfloat16)
+    loads[1].wait()
+
+    tile = min(256, act.shape[1])
+
+    def hidden(index, carry):
+        cut = pl.ds(pl.multiple_of(index * tile, tile), tile)
+        values = jnp.dot(normed[...], w_in[:, cut], preferred_element_type=jnp.float32)
+        act[:, cut] = jax.nn.gelu(values).astype(jnp.bfloat16)
+        return carry
+
+    lax.fori_loop(0, act.shape[1] // tile, hidden, 0)
+    loads[2].wait()
+    mlp = scatter_products(3, act, w_out, sent2, summed2)
+    gathered2[me] = (own[...] + mlp).astype(jnp.bfloat16)
+    gather(4, gathered2)
+    for index in range(count):
+        normed[:, index * width : (index + 1) * width] = gathered2[index]
+    loads[3].wait()
+    cols[...] = jnp.dot(normed[...], split[...], preferred_element_type=jnp.float32)
+    for index in range(count):
+        sent3[index] = cols[index * own_count : (index + 1) * own_count].astype(jnp.bfloat16)
+
+    def last(step, carry):
+        peer = lax.rem(me + step, count)
+        copy_to(5, peer, sent3.at[peer], landed3).start()
+        return carry
+
+    lax.fori_loop(1, count, last, 0)
+    landed3[me] = sent3[me]
+    wait_from(5, landed3)
+    pieces_ref[...] = landed3[...]
+    wait_sent(0, lambda peer: blocks_ref.at[peer], landed)
+    wait_sent(1, lambda peer: sent.at[peer], summed)
+    wait_sent(2, lambda peer: gathered.at[me], gathered)
+    wait_sent(3, lambda peer: sent2.at[peer], summed2)
+    wait_sent(4, lambda peer: gathered2.at[me], gathered2)
+    wait_sent(5, lambda peer: sent3.at[peer], landed3)
+
+
+def coarse_in_one(blocks, merge_two, mlp_in, mlp_out, split_weight):
+    count, own_count, depth = blocks.shape
+    tokens, top = count * own_count, merge_two.shape[1]
+    width, hidden, split_width = top // count, mlp_in.shape[1], split_weight.shape[1]
+    low = jnp.bfloat16
+    whole = pl.BlockSpec(memory_space=pltpu.VMEM)
+    apart = pl.BlockSpec(memory_space=pl.ANY)
+    return pl.pallas_call(
+        coarse_kernel,
+        out_shape=jax.ShapeDtypeStruct((count, own_count, split_width), low),
+        in_specs=[whole, apart, apart, apart, apart],
+        out_specs=whole,
+        scratch_shapes=[
+            pltpu.VMEM(merge_two.shape, low),
+            pltpu.VMEM(mlp_in.shape, low),
+            pltpu.VMEM(mlp_out.shape, low),
+            pltpu.VMEM(split_weight.shape, low),
+            pltpu.VMEM((count, own_count, depth), low),
+            pltpu.VMEM((tokens, depth), jnp.float32),
+            pltpu.VMEM((count, tokens, width), low),
+            pltpu.VMEM((count, tokens, width), low),
+            pltpu.VMEM((tokens, width), jnp.float32),
+            pltpu.VMEM((count, tokens, width), low),
+            pltpu.VMEM((tokens, top), low),
+            pltpu.VMEM((tokens, hidden), low),
+            pltpu.VMEM((count, tokens, width), low),
+            pltpu.VMEM((count, tokens, width), low),
+            pltpu.VMEM((count, tokens, width), low),
+            pltpu.VMEM((tokens, split_width), jnp.float32),
+            pltpu.VMEM((count, own_count, split_width), low),
+            pltpu.VMEM((count, own_count, split_width), low),
+            pltpu.SemaphoreType.DMA((4,)),
+            pltpu.SemaphoreType.DMA((6, count)),
+            pltpu.SemaphoreType.DMA((6, count)),
+        ],
+        compiler_params=pltpu.CompilerParams(
+            collective_id=0, has_side_effects=True, vmem_limit_bytes=40 * 1024 * 1024
+        ),
+    )(blocks, merge_two, mlp_in, mlp_out, split_weight)
+
+
+def coarse_apart(normed2, merge_two, mlp_in, mlp_out, split_weight):
+    own_count = normed2.shape[0]
+    feature_parts = lax.all_to_all(normed2, "lon", split_axis=1, concat_axis=0, tiled=True)
+    partial_value = jnp.dot(feature_parts, merge_two, preferred_element_type=jnp.float32)
+    merged2 = lax.psum(partial_value.astype(jnp.bfloat16), "lon").astype(jnp.float32)
+    normed3 = layer_norm(merged2).astype(jnp.bfloat16)
+    act = jax.nn.gelu(jnp.dot(normed3, mlp_in, preferred_element_type=jnp.float32)).astype(
+        jnp.bfloat16
+    )
+    mlp_own = lax.psum_scatter(
+        jnp.dot(act, mlp_out, preferred_element_type=jnp.float32).astype(jnp.bfloat16),
+        "lon",
+        scatter_dimension=0,
+        tiled=True,
+    ).astype(jnp.float32)
+    own_merged = lax.dynamic_slice_in_dim(merged2, lax.axis_index("lon") * own_count, own_count, 0)
+    coarse = (own_merged + mlp_own).astype(jnp.bfloat16)
+    split_cols = jnp.dot(
+        lax.all_gather(coarse, "lon", axis=0, tiled=True),
+        split_weight,
+        preferred_element_type=jnp.float32,
+    ).astype(jnp.bfloat16)
+    return lax.all_to_all(split_cols, "lon", split_axis=0, concat_axis=1, tiled=True)
 
 
 def on_device(
@@ -91,28 +319,13 @@
     ).astype(jnp.bfloat16)
     merged1 = merged1.reshape(levels, rows // 2, cols // 2, MID)
     normed2 = layer_norm(cat_four(merged1.astype(jnp.float32))).astype(jnp.bfloat16)
-    own_count = normed2.shape[0]
-    feature_parts = lax.all_to_all(normed2, "lon", split_axis=1, concat_axis=0, tiled=True)
-    partial_value = jnp.dot(feature_parts, merge_two, preferred_element_type=jnp.float32)
-    merged2 = lax.psum(partial_value.astype(jnp.bfloat16), "lon").astype(jnp.float32)
-    normed3 = layer_norm(merged2).astype(jnp.bfloat16)
-    act = jax.nn.gelu(jnp.dot(normed3, mlp_in, preferred_element_type=jnp.float32)).astype(
-        jnp.bfloat16
-    )
-    mlp_own = lax.psum_scatter(
-        jnp.dot(act, mlp_out, preferred_element_type=jnp.float32).astype(jnp.bfloat16),
-        "lon",
-        scatter_dimension=0,
-        tiled=True,
-    ).astype(jnp.float32)
-    own_merged = lax.dynamic_slice_in_dim(merged2, lax.axis_index("lon") * own_count, own_count, 0)
-    coarse = (own_merged + mlp_own).astype(jnp.bfloat16)
-    split_cols = jnp.dot(
-        lax.all_gather(coarse, "lon", axis=0, tiled=True),
-        split_weight,
-        preferred_element_type=jnp.float32,
-    ).astype(jnp.bfloat16)
-    pieces = lax.all_to_all(split_cols, "lon", split_axis=0, concat_axis=1, tiled=True)
+    count = lax.axis_size("lon")
+    if merge_two.shape[1] % (count * 128) == 0:
+        blocks = normed2.reshape(normed2.shape[0], count, -1).transpose(1, 0, 2)
+        pieces = coarse_in_one(blocks, merge_two, mlp_in, mlp_out, split_weight)
+        pieces = pieces.transpose(1, 0, 2)
+    else:
+        pieces = coarse_apart(normed2, merge_two, mlp_in, mlp_out, split_weight)
     pieces = pieces.reshape(levels, rows // 4, cols // 4, 2, 2, MID).transpose(0, 1, 3, 2, 4, 5)
     pieces = pieces.reshape(levels, rows // 2, cols // 2, MID)
     mid_out = merged1.astype(jnp.float32) + pieces.astype(jnp.float32)

time: 266 us -> 167 us (0.63)
  Pallas kernels: 0 us -> 75.7 us
  blocking collectives: 78.7 us -> 8.81 us
  waiting for transfers between devices: 96.2 us -> 27.2 us
  matrix products: 23.6 us -> 10.2 us
  starting transfers between devices: 18 us -> 9.19 us
  local copies, waits for them, and re-layouts: 24.9 us -> 17.6 us
  other arithmetic: 8.32 us -> 3.65 us
    pallas_call x0 -> x1, Pallas kernels: none -> 75.7 us  [coarse_in_one(): pl.pallas_call(coarse_kernel, out_shape=jax.ShapeDtypeStruct((count, own_...]
    psum x1 -> x0, waiting for transfers between devices: 70.7 us -> none  [on_device(): lax.psum(partial_value.astype(jnp.bfloat16), 'lon').astype(jnp.float32)]
    all_gather x1 -> x0, blocking collectives: 33 us -> none  [on_device(): lax.all_gather(coarse, 'lon', axis=0, tiled=True)]
    unnamed x1 -> x0, blocking collectives: 26.7 us -> none
    all_to_all x1 -> x0, blocking collectives: 10.2 us -> none  [on_device(): lax.all_to_all(normed2, 'lon', split_axis=1, concat_axis=0, tiled=True)]
    dot_general x3 -> x0, matrix products: 9.67 us -> none  [the longest x1 6.12 us: on_device(): jnp.dot(act, mlp_out, preferred_element_type=jnp.float32)]
    all_gather x1, waiting for transfers between devices: 0.02 us -> 8.06 us  [on_device(): lax.all_gather(merge_one, 'lat', axis=1, tiled=True)]
    all_to_all x1 -> x0, waiting for transfers between devices: 7.67 us -> none  [on_device(): lax.all_to_all(split_cols, 'lon', split_axis=0, concat_axis=1, tiled=True)]
  transfers between devices with their start and end apart: 10 -> 6, of which waited for: 7 -> 5; matrix products, arithmetic and copies ran while one was open for 13% -> 11% of each run, Pallas kernels for 0% -> 0%
where the time goes in v1:
time: 167 us
  Pallas kernels  75.7 us (45%)
  waiting for transfers between devices  27.2 us (16%)
  local copies, waits for them, and re-layouts  17.6 us (11%)
  between operations  14.4 us (9%)
  matrix products  10.2 us (6%)
  starting transfers between devices  9.19 us (6%)
  blocking collectives  8.81 us (5%)
  other arithmetic  3.65 us (2%)
    pallas_call x1, Pallas kernels, coarse_in_one(): pl.pallas_call(coarse_kernel, out_shape=jax.ShapeDtypeStruct((count, own_...  75.7 us
    ppermute x4, waiting for transfers between devices, from_behind(): return lax.ppermute(value, axis, pairs)  16.7 us
    ppermute x4, starting transfers between devices, from_behind(): return lax.ppermute(value, axis, pairs)  9.12 us
    all_gather x1, blocking collectives, on_device(): lax.all_gather(proj_weight, 'lat', axis=1, tiled=True)  8.81 us
    unnamed x17, local copies, waits for them, and re-layouts  8.58 us
    all_gather x1, waiting for transfers between devices, on_device(): lax.all_gather(merge_one, 'lat', axis=1, tiled=True)  8.06 us
  transfers between devices with their start and end apart: 6, of which 5 were waited for; matrix products, arithmetic and copies ran while one was open for 11% of the time, Pallas kernels for 0%

profile of v1, /device:TPU:0, one launch (start us, length us, event | category | flops | bytes accessed | tf_op | source)
XLA Modules:
  0.0 166.8 jit_solution(15555068618184625686)
XLA Ops:
  7.2 0.7 all-gather.3.cloned.1.call-update
  7.9 0.7 all-gather.5.cloned.1.call-update
  8.6 1.2 fusion.38
  9.8 6.1 %collective-permute-start = (bf16[2,12,6,512]{3,0,2,1:T(2,128)(2,1)S(1)}, bf16[2,12,6,512]{3,0,2,1:T(2,128)(2,1)S(1)}, u32[]{:S(2)}, u32[]{:S(2)}) collective-permute-start(bf16[2,12,6,512]{3,0,2,1:T(2,128)(2,1)S(1)} %get-tuple-element.14), channel_id=1, source_target_pairs={{0,7},{1,0},{2,1},{3,2},{4,3},{5,4},{6,5},{7,6},{8,15},{9,8},{10,9... | collective-permute-start | bytes 442376 | tf_op jit(solution)/shard_map/ppermute | solution.py:21
  16.2 8.8 %all_gather.10 = bf16[512,512]{1,0:T(8,128)(2,1)S(1)} all-gather(bf16[512,128]{1,0:T(8,128)(2,1)} %param.10), channel_id=1, replica_groups=mesh['lat'=4,'lon'=8] {'lat'}, dimensions={1}, use_global_device_ids=true | all-gather | bytes 655360 | tf_op jit(solution)/shard_map/all_gather | solution.py:271
  25.1 1.9 %collective-permute-start.1 = (bf16[2,3,12,512]{3,0,2,1:T(2,128)(2,1)S(1)}, bf16[2,3,12,512]{3,0,2,1:T(2,128)(2,1)S(1)}, u32[]{:S(2)}, u32[]{:S(2)}) collective-permute-start(bf16[2,3,12,512]{3,0,2,1:T(2,128)(2,1)S(1)} %pad_maximum_fusion.1), channel_id=1, source_target_pairs={{0,24},{8,0},{16,8},{24,16},{1,25},{9,1},{17,9},{25,17},{2,26},{10... | collective-permute-start | bytes 221192 | tf_op jit(solution)/shard_map/ppermute | solution.py:21
  27.0 0.3 fusion.18
  27.3 3.0 %collective-permute-done.1 = bf16[2,3,12,512]{3,0,2,1:T(2,128)(2,1)S(1)} collective-permute-done((bf16[2,3,12,512]{3,0,2,1:T(2,128)(2,1)S(1)}, bf16[2,3,12,512]{3,0,2,1:T(2,128)(2,1)S(1)}, u32[]{:S(2)}, u32[]{:S(2)}) %collective-permute-start.1) | collective-permute-done | bytes 73760 | tf_op jit(solution)/shard_map/ppermute | solution.py:21
  30.3 0.4 fusion.36
  30.7 0.2 copy.78
  30.9 0.6 multiply_reduce_fusion.1
  31.5 0.2 copy.81
  31.9 0.3 maximum_convert_fusion
  32.5 1.0 all-gather.3.cloned.1.call-done
  33.5 2.1 %convolution_convert_fusion = bf16[288,1536]{1,0:T(8,128)(2,1)S(1)} fusion(bf16[512,1536]{1,0:T(8,128)(2,1)} %all-gather.3.cloned.1.call-done, f32[288,512]{1,0:T(8,128)S(1)} %reshape.175, f32[288]{0:T(512)S(1)} %rsqrt.34, f32[288]{0:T(512)S(1)} %div.39), kind=kOutput, calls=%fused_computation.1 | convolution fusion | flops 453869568 | bytes 3049728 | tf_op jit(solution)/shard_map/dot_general | solution.py:278
  35.6 1.1 reshape.167
  36.6 0.3 copy.82
  37.0 0.3 fusion.37
  37.3 0.4 copy.103
  37.7 0.4 copy.104
  38.1 0.4 copy.102
  38.5 2.4 %fusion.39 = (f32[2,8,144]{2,1,0:T(8,128)S(1)}, f32[2,8,144,144]{2,3,1,0:T(8,128)}) fusion(pred[2,144,144]{1,2,0:T(8,128)(4,1)S(1)} %broadcast_compare_fusion, bf16[2,144,1,8,64]{1,4,3,0,2:T(8,128)(2,1)S(1)} %copy.104, bf16[2,144,1,8,64]{1,4,3,0,2:T(8,128)(2,1)S(1)} %copy.103), kind=kOutput, calls=%fused_computation.59 | convolution fusion | flops 43794576 | bytes 1967616 | tf_op jit(solution)/shard_map/sub | solution.py:298
  40.9 2.3 %fusion.2 = bf16[2,144,8,64]{1,3,2,0:T(8,128)(2,1)S(1)} fusion(f32[2,8,144,144]{2,3,1,0:T(8,128)} %get-tuple-element.16, f32[2,8,144]{2,1,0:T(8,128)S(1)} %get-tuple-element.15, bf16[2,144,1,8,64]{1,4,3,0,2:T(8,128)(2,1)S(1)} %copy.102), kind=kOutput, calls=%fused_computation.7 | convolution fusion | flops 43278336 | bytes 1926144 | tf_op jit(solution)/shard_map/whqk,wkhd->wqhd/dot_general | solution.py:300
  43.2 0.5 copy.87
  43.8 0.3 reshape.169
  44.2 0.3 convolution_convert_fusion.2
  44.6 0.2 collective-permute-start.2
  44.9 6.0 %collective-permute-done.2 = bf16[2,3,12,512]{3,2,1,0:T(8,128)(2,1)S(1)} collective-permute-done((bf16[2,3,12,512]{3,2,1,0:T(8,128)(2,1)S(1)}, bf16[2,3,12,512]{3,2,1,0:T(8,128)(2,1)S(1)}, u32[]{:S(2)}, u32[]{:S(2)}) %collective-permute-start.2) | collective-permute-done | bytes 73760 | tf_op jit(solution)/shard_map/ppermute | solution.py:21
  51.0 0.9 collective-permute-start.3
  51.9 7.7 %collective-permute-done.3 = bf16[2,12,6,512]{3,2,1,0:T(8,128)(2,1)S(1)} collective-permute-done((bf16[2,12,6,512]{3,2,1,0:T(8,128)(2,1)S(1)}, bf16[2,12,6,512]{3,2,1,0:T(8,128)(2,1)S(1)}, u32[]{:S(2)}, u32[]{:S(2)}) %collective-permute-start.3) | collective-permute-done | bytes 147488 | tf_op jit(solution)/shard_map/ppermute | solution.py:21
  59.8 0.5 copy.99
  60.3 0.3 copy.90
  60.6 0.2 reduce_sum.66
  61.0 0.5 multiply_reduce_fusion
  61.7 0.5 reshape.173
  62.3 8.1 %all-gather.5.cloned.1.call-done = bf16[2048,1024]{1,0:T(8,128)(2,1)} async-done(((bf16[2048,256]{1,0:T(8,128)(2,1)}), bf16[2048,1024]{1,0:T(8,128)(2,1)}) %all-gather.5.cloned.1.call-update) | async-done | bytes 4194320 | tf_op jit(solution)/shard_map/all_gather | solution.py:317
  70.3 3.1 %fusion.6 = f32[72,1024]{1,0:T(8,128)S(1)} fusion(bf16[2048,1024]{1,0:T(8,128)(2,1)} %all-gather.5.cloned.1.call-done, f32[72,2048]{1,0:T(8,128)S(1)} %reshape.173, f32[72]{0:T(128)S(1)} %rsqrt.36, f32[72]{0:T(128)S(1)} %div.46), kind=kOutput, calls=%fused_computation.13 | convolution fusion | flops 302579712 | bytes 5079616 | tf_op jit(solution)/shard_map/dot_general | solution.py:315
  73.8 0.7 copy.123
  74.6 0.3 multiply_reduce_fusion.2
  75.1 1.2 reshape.174
  76.5 2.2 %copy-done = bf16[2048,1024]{1,0:T(8,128)(2,1)S(1)} copy-done((bf16[2048,1024]{1,0:T(8,128)(2,1)S(1)}, bf16[2048,1024]{1,0:T(8,128)(2,1)}, u32[]{:S(2)}) %copy-start) | copy-done | bytes 4194328
  78.7 2.2 %copy-done.1 = bf16[1024,2048]{1,0:T(8,128)(2,1)S(1)} copy-done((bf16[1024,2048]{1,0:T(8,128)(2,1)S(1)}, bf16[1024,2048]{1,0:T(8,128)(2,1)}, u32[]{:S(2)}) %copy-start.1) | copy-done | bytes 4194328
  80.9 1.6 copy-done.3
  82.5 75.7 %shard_map.95 = bf16[8,18,512]{2,1,0:T(8,128)(2,1)S(1)} custom-call(bf16[8,18,512]{2,1,0:T(8,128)(2,1)S(1)} %fusion.19.blocks_ref, bf16[512,2048]{1,0:T(8,128)(2,1)S(1)} %copy-done.2, bf16[2048,1024]{1,0:T(8,128)(2,1)S(1)} %copy-done, bf16[1024,2048]{1,0:T(8,128)(2,1)S(1)} %copy-done.1, bf16[2048,512]{1,0:T(8,128)(2,1)S(1)} %copy-done.3), custom_call_target="tpu_custom_call" | custom-call | tf_op jit(solution)/shard_map/pallas_call | solution.py:204
  158.2 0.2 copy.96
  158.4 0.2 reshape.179
  158.6 0.2 copy.97
  159.0 0.9 copy.100
  (46 shorter events, 2.7 us)
Async XLA Ops:
  7.2 26.3 %all-gather.3.cloned.1.call-start = ((), (), s32[]{:S(2)}) async-start(), calls=%async_computation | async-start | bytes 1966080 | tf_op jit(solution)/shard_map/all_gather | solution.py:270
  7.9 62.4 %all-gather.5.cloned.1.call-start = ((), (), s32[]{:S(2)}) async-start(), calls=%async_computation.1 | async-start | bytes 5242880 | tf_op jit(solution)/shard_map/all_gather | solution.py:317
  9.8 15.2 %collective-permute-start = (bf16[2,12,6,512]{3,0,2,1:T(2,128)(2,1)S(1)}, bf16[2,12,6,512]{3,0,2,1:T(2,128)(2,1)S(1)}, u32[]{:S(2)}, u32[]{:S(2)}) collective-permute-start(bf16[2,12,6,512]{3,0,2,1:T(2,128)(2,1)S(1)} %get-tuple-element.14), channel_id=1, source_target_pairs={{0,7},{1,0},{2,1},{3,2},{4,3},{5,4},{6,5},{7,6},{8,15},{9,8},{10,9... | collective-permute-start | bytes 442376 | tf_op jit(solution)/shard_map/ppermute | solution.py:21
  25.1 5.2 %collective-permute-start.1 = (bf16[2,3,12,512]{3,0,2,1:T(2,128)(2,1)S(1)}, bf16[2,3,12,512]{3,0,2,1:T(2,128)(2,1)S(1)}, u32[]{:S(2)}, u32[]{:S(2)}) collective-permute-start(bf16[2,3,12,512]{3,0,2,1:T(2,128)(2,1)S(1)} %pad_maximum_fusion.1), channel_id=1, source_target_pairs={{0,24},{8,0},{16,8},{24,16},{1,25},{9,1},{17,9},{25,17},{2,26},{10... | collective-permute-start | bytes 221192 | tf_op jit(solution)/shard_map/ppermute | solution.py:21
  44.1 15.6 %copy-start.5 = (bf16[2,12,12,512]{3,0,2,1:T(2,128)(2,1)S(1)}, bf16[2,12,12,512]{3,0,2,1:T(2,128)(2,1)}, u32[]{:S(2)}) copy-start(bf16[2,12,12,512]{3,0,2,1:T(2,128)(2,1)} %param.8) | copy-start | bytes 884740
  44.6 6.3 %collective-permute-start.2 = (bf16[2,3,12,512]{3,2,1,0:T(8,128)(2,1)S(1)}, bf16[2,3,12,512]{3,2,1,0:T(8,128)(2,1)S(1)}, u32[]{:S(2)}, u32[]{:S(2)}) collective-permute-start(bf16[2,3,12,512]{3,2,1,0:T(8,128)(2,1)S(1)} %slice.49), channel_id=1, source_target_pairs={{0,8},{8,16},{16,24},{24,0},{1,9},{9,17},{17,25},{25,1},{2,10},{10... | collective-permute-start | bytes 221192 | tf_op jit(solution)/shard_map/ppermute | solution.py:21
  51.0 8.6 %collective-permute-start.3 = (bf16[2,12,6,512]{3,2,1,0:T(8,128)(2,1)S(1)}, bf16[2,12,6,512]{3,2,1,0:T(8,128)(2,1)S(1)}, u32[]{:S(2)}, u32[]{:S(2)}) collective-permute-start(bf16[2,12,6,512]{3,2,1,0:T(8,128)(2,1)S(1)} %fusion.20), channel_id=1, source_target_pairs={{0,1},{1,2},{2,3},{3,4},{4,5},{5,6},{6,7},{7,0},{8,9},{9,10},{10,1... | collective-permute-start | bytes 442376 | tf_op jit(solution)/shard_map/ppermute | solution.py:21
  60.3 13.2 %copy-start.4 = (f32[2,12,12,512]{3,0,2,1:T(2,128)}, f32[2,12,12,512]{3,0,2,1:T(2,128)S(1)}, u32[]{:S(2)}) copy-start(f32[2,12,12,512]{3,0,2,1:T(2,128)S(1)} %copy.99) | copy-start | bytes 1769476
  73.5 3.1 %copy-start.2 = (bf16[512,2048]{1,0:T(8,128)(2,1)S(1)}, bf16[512,2048]{1,0:T(8,128)(2,1)}, u32[]{:S(2)}) copy-start(bf16[512,2048]{1,0:T(8,128)(2,1)} %two_hbm.1) | copy-start | bytes 6291460
  76.5 2.2 %copy-start = (bf16[2048,1024]{1,0:T(8,128)(2,1)S(1)}, bf16[2048,1024]{1,0:T(8,128)(2,1)}, u32[]{:S(2)}) copy-start(bf16[2048,1024]{1,0:T(8,128)(2,1)} %in_hbm.1) | copy-start | bytes 12582916
  78.7 2.2 %copy-start.1 = (bf16[1024,2048]{1,0:T(8,128)(2,1)S(1)}, bf16[1024,2048]{1,0:T(8,128)(2,1)}, u32[]{:S(2)}) copy-start(bf16[1024,2048]{1,0:T(8,128)(2,1)} %out_hbm.1) | copy-start | bytes 12582916
  80.9 1.6 copy-start.3
Sparse Core Ops, SparseCore 0:
  9.5 23.8 all-gather.2
  35.0 35.2 all-gather.4

commit v2 on v1

--- a/solution.py
+++ b/solution.py
@@ -1,3 +1,4 @@
+import functools
 import math
 
 import jax
@@ -13,12 +14,6 @@
 WIN_C = 12
 SHIFT_R = 3
 SHIFT_C = 6
-
-
-def from_behind(value, axis, steps):
-    count = lax.axis_size(axis)
-    pairs = [(source, (source + steps) % count) for source in range(count)]
-    return lax.ppermute(value, axis, pairs)
 
 
 def layer_norm(values):
@@ -230,7 +225,7 @@
             pltpu.SemaphoreType.DMA((6, count)),
         ],
         compiler_params=pltpu.CompilerParams(
-            collective_id=0, has_side_effects=True, vmem_limit_bytes=40 * 1024 * 1024
+            collective_id=0, has_side_effects=True, vmem_limit_bytes=60 * 1024 * 1024
         ),
     )(blocks, merge_two, mlp_in, mlp_out, split_weight)
 
@@ -260,20 +255,150 @@
     return lax.all_to_all(split_cols, "lon", split_axis=0, concat_axis=1, tiled=True)
 
 
+def halo_kernel(direction, shards, *refs):
+    edges, weights = refs[:3], refs[3 : 3 + shards]
+    came, wholes = refs[3 + shards : 6 + shards], refs[6 + shards : 6 + 2 * shards]
+    edge_send, edge_recv, own_sem, weight_send, weight_recv = refs[6 + 2 * shards :]
+    lat_count, lon_count = lax.axis_size("lat"), lax.axis_size("lon")
+    row, col = lax.axis_index("lat"), lax.axis_index("lon")
+    mesh = pl.DeviceIdType.MESH
+
+    def beside(sign):
+        next_row = lax.rem(row + sign + lat_count, lat_count)
+        next_col = lax.rem(col + sign + lon_count, lon_count)
+        return (next_row, col), (row, next_col), (next_row, next_col)
+
+    other_core = row + 1 - 2 * lax.rem(row, 2)
+    other_chip = lax.rem(row + 2, 4)
+    partners = beside(1) + beside(-1)
+    if shards:
+        partners += ((other_core, col), (other_chip, col))
+    barrier = pltpu.get_barrier_semaphore()
+    for partner in partners:
+        pl.semaphore_signal(barrier, inc=1, device_id=partner, device_id_type=mesh)
+    pl.semaphore_wait(barrier, len(partners))
+
+    copies = []
+    for index, target in enumerate(beside(direction)):
+        copies.append(
+            pltpu.make_async_remote_copy(
+                src_ref=edges[index],
+                dst_ref=came[index],
+                send_sem=edge_send.at[index],
+                recv_sem=edge_recv.at[index],
+                device_id=target,
+                device_id_type=mesh,
+            )
+        )
+    for copy in copies:
+        copy.start()
+
+    def columns(index, owner):
+        width = weights[index].shape[1]
+        return wholes[index].at[:, pl.ds(pl.multiple_of(owner * width, width), width)]
+
+    relays = []
+    for index in range(shards):
+        across = []
+        for kind, target in enumerate((other_chip, other_core)):
+            across.append(
+                pltpu.make_async_remote_copy(
+                    src_ref=weights[index],
+                    dst_ref=columns(index, row),
+                    send_sem=weight_send.at[index, kind],
+                    recv_sem=weight_recv.at[index, kind],
+                    device_id=(target, col),
+                    device_id_type=mesh,
+                )
+            )
+        for copy in across:
+            copy.start()
+        pltpu.make_async_copy(weights[index], columns(index, row), own_sem.at[index]).start()
+        relays.append(across)
+    for index in range(shards):
+        relays[index][0].wait_recv()
+        relay = pltpu.make_async_remote_copy(
+            src_ref=columns(index, other_chip),
+            dst_ref=columns(index, other_chip),
+            send_sem=weight_send.at[index, 2],
+            recv_sem=weight_recv.at[index, 2],
+            device_id=(other_core, col),
+            device_id_type=mesh,
+        )
+        relay.start()
+        relays[index].append(relay)
+    for index in range(shards):
+        relays[index][0].wait_send()
+        relays[index][1].wait()
+        relays[index][2].wait()
+        pltpu.make_async_copy(weights[index], columns(index, row), own_sem.at[index]).wait()
+    for copy in copies:
+        copy.wait()
+
+
+def exchange(edges, direction, weights, identity):
+    whole = pl.BlockSpec(memory_space=pltpu.VMEM)
+    shards = len(weights)
+    outs = [jax.ShapeDtypeStruct(edge.shape, edge.dtype) for edge in edges]
+    outs += [
+        jax.ShapeDtypeStruct((part.shape[0], 4 * part.shape[1]), part.dtype) for part in weights
+    ]
+    return pl.pallas_call(
+        functools.partial(halo_kernel, direction, shards),
+        out_shape=outs,
+        in_specs=[whole] * (3 + shards),
+        out_specs=[whole] * (3 + shards),
+        scratch_shapes=[
+            pltpu.SemaphoreType.DMA((3,)),
+            pltpu.SemaphoreType.DMA((3,)),
+            pltpu.SemaphoreType.DMA((max(shards, 1),)),
+            pltpu.SemaphoreType.DMA((max(shards, 1), 3)),
+            pltpu.SemaphoreType.DMA((max(shards, 1), 3)),
+        ],
+        compiler_params=pltpu.CompilerParams(collective_id=identity, has_side_effects=True),
+    )(*edges, *weights)
+
+
+def lat_swap(value, mask):
+    return lax.ppermute(value, "lat", [(index, index ^ mask) for index in range(4)])
+
+
+def in_owner_order(parts):
+    index = lax.axis_index("lat")
+    odd, high = index % 2 == 1, index >= 2
+    a, b, c, d = parts
+    a, b = jnp.where(odd, b, a), jnp.where(odd, a, b)
+    c, d = jnp.where(odd, d, c), jnp.where(odd, c, d)
+    a, c = jnp.where(high, c, a), jnp.where(high, a, c)
+    b, d = jnp.where(high, d, b), jnp.where(high, b, d)
+    return jnp.concatenate((a, b, c, d), axis=-1)
+
+
 def on_device(
     fine_tokens, qkv_weight, proj_weight, merge_one, merge_two, mlp_in, mlp_out, split_weight
 ):
     levels, rows, cols, width = fine_tokens.shape
     lat_count = lax.axis_size("lat")
     head_dim = width // HEADS
-    full_qkv, full_proj = (
-        lax.all_gather(qkv_weight, "lat", axis=1, tiled=True),
-        lax.all_gather(proj_weight, "lat", axis=1, tiled=True),
-    )
-    came = from_behind(fine_tokens[:, :, :SHIFT_C], "lon", -1)
-    col_moved = jnp.concatenate([fine_tokens[:, :, SHIFT_C:], came], axis=2)
-    came = from_behind(col_moved[:, :SHIFT_R], "lat", -1)
-    moved = jnp.concatenate([col_moved[:, SHIFT_R:], came], axis=1)
+    edges = (
+        fine_tokens[:, :SHIFT_R, SHIFT_C:],
+        fine_tokens[:, SHIFT_R:, :SHIFT_C],
+        fine_tokens[:, :SHIFT_R, :SHIFT_C],
+    )
+    if lat_count == 4:
+        row_came, col_came, both_came, full_qkv, full_proj = exchange(
+            edges, -1, (qkv_weight, proj_weight), 1
+        )
+        merge_one, row_came = lax.optimization_barrier((merge_one, row_came))
+        merge_far = lat_swap(merge_one, 2)
+        merge_parts = (merge_one, lat_swap(merge_one, 1), merge_far, lat_swap(merge_far, 1))
+    else:
+        row_came, col_came, both_came = exchange(edges, -1, (), 1)
+        full_qkv = lax.all_gather(qkv_weight, "lat", axis=1, tiled=True)
+        full_proj = lax.all_gather(proj_weight, "lat", axis=1, tiled=True)
+    upper = jnp.concatenate([fine_tokens[:, SHIFT_R:, SHIFT_C:], col_came], axis=2)
+    lower = jnp.concatenate([row_came, both_came], axis=2)
+    moved = jnp.concatenate([upper, lower], axis=1)
     normed = layer_norm(moved.astype(jnp.float32)).astype(jnp.bfloat16).reshape(-1, width)
     qkv = jnp.dot(normed, full_qkv, preferred_element_type=jnp.float32).astype(jnp.bfloat16)
     row_wins = rows // WIN_R
@@ -306,17 +431,28 @@
     heads_out = heads_out.transpose(2, 0, 3, 1, 4, 5).reshape(-1, width)
     attn = jnp.dot(heads_out, full_proj, preferred_element_type=jnp.float32).astype(jnp.bfloat16)
     attn = attn.reshape(levels, rows, cols, width)
-    came = from_behind(attn[:, rows - SHIFT_R :], "lat", 1)
-    row_back = jnp.concatenate([came, attn[:, : rows - SHIFT_R]], axis=1)
-    came = from_behind(row_back[:, :, cols - SHIFT_C :], "lon", 1)
-    back = jnp.concatenate([came, row_back[:, :, : cols - SHIFT_C]], axis=2)
+    edges = (
+        attn[:, rows - SHIFT_R :, : cols - SHIFT_C],
+        attn[:, : rows - SHIFT_R, cols - SHIFT_C :],
+        attn[:, rows - SHIFT_R :, cols - SHIFT_C :],
+    )
+    row_came, col_came, both_came = exchange(edges, 1, (), 2)
+    upper = jnp.concatenate([both_came, row_came], axis=2)
+    lower = jnp.concatenate([col_came, attn[:, : rows - SHIFT_R, : cols - SHIFT_C]], axis=2)
+    back = jnp.concatenate([upper, lower], axis=1)
     fine_out = fine_tokens.astype(jnp.float32) + back.astype(jnp.float32)
     normed1 = layer_norm(cat_four(fine_out)).astype(jnp.bfloat16)
-    merged1 = jnp.dot(
-        normed1,
-        lax.all_gather(merge_one, "lat", axis=1, tiled=True),
-        preferred_element_type=jnp.float32,
-    ).astype(jnp.bfloat16)
+    if lat_count == 4:
+        merged1 = in_owner_order(
+            [
+                jnp.dot(normed1, part, preferred_element_type=jnp.float32).astype(jnp.bfloat16)
+                for part in merge_parts
+            ]
+        )
+    else:
+        merge_all = lax.all_gather(merge_one, "lat", axis=1, tiled=True)
+        merged1 = jnp.dot(normed1, merge_all, preferred_element_type=jnp.float32)
+        merged1 = merged1.astype(jnp.bfloat16)
     merged1 = merged1.reshape(levels, rows // 2, cols // 2, MID)
     normed2 = layer_norm(cat_four(merged1.astype(jnp.float32))).astype(jnp.bfloat16)
     count = lax.axis_size("lon")

time: 167 us -> 147 us (0.88)
  Pallas kernels: 75.7 us -> 112 us
  waiting for transfers between devices: 27.2 us -> 0.01 us
  between operations: 14.4 us -> 1.08 us
  blocking collectives: 8.81 us -> 0 us
  starting transfers between devices: 9.19 us -> 1.03 us
  other arithmetic: 3.65 us -> 8.07 us
  local copies, waits for them, and re-layouts: 17.6 us -> 13.5 us
    pallas_call x0 -> x2, Pallas kernels: none -> 36.7 us  [exchange(): pl.pallas_call(functools.partial(halo_kernel, direction, shards), out_sha...]
    ppermute x4 -> x3, waiting for transfers between devices: 16.7 us -> 0.01 us  [lat_swap(): lax.ppermute(value, 'lat', [(index, index ^ mask) for index in range(4)])]
    all_gather x2 -> x0, waiting for transfers between devices: 9.06 us -> none  [the longest x1 8.06 us: on_device(): lax.all_gather(merge_one, 'lat', axis=1, tiled=True)]
    all_gather x1 -> x0, blocking collectives: 8.81 us -> none  [on_device(): lax.all_gather(proj_weight, 'lat', axis=1, tiled=True)]
    ppermute x4 -> x3, starting transfers between devices: 9.12 us -> 1.03 us  [lat_swap(): lax.ppermute(value, 'lat', [(index, index ^ mask) for index in range(4)])]
    unnamed x17, local copies, waits for them, and re-layouts: 8.58 us -> 4.59 us
    slice x3 -> x4, local copies, waits for them, and re-layouts: 1.22 us -> 3.31 us  [the longest x1 1.11 us: on_device(): fine_tokens[:, SHIFT_R:, SHIFT_C:]]
    dot_general x1 -> x4, matrix products: 3.11 us -> 3.68 us  [on_device(): jnp.dot(normed1, part, preferred_element_type=jnp.float32)]
  transfers between devices with their start and end apart: 6 -> 3, of which waited for: 5 -> 0; matrix products, arithmetic and copies ran while one was open for 11% -> 16% of each run, Pallas kernels for 0% -> 8%
where the time goes in v2:
time: 147 us; the launch traced here: 146 us
  Pallas kernels  112 us (76%)
  local copies, waits for them, and re-layouts  13.5 us (9%)
  matrix products  10.5 us (7%)
  other arithmetic  8.07 us (5%)
    pallas_call x1, Pallas kernels, coarse_in_one(): pl.pallas_call(coarse_kernel, out_shape=jax.ShapeDtypeStruct((count, own_...  75.1 us
    pallas_call x2, Pallas kernels, exchange(): pl.pallas_call(functools.partial(halo_kernel, direction, shards), out_sha...  36.7 us
    unnamed x17, local copies, waits for them, and re-layouts  4.59 us
    dot_general x4, matrix products, on_device(): jnp.dot(normed1, part, preferred_element_type=jnp.float32)  3.68 us
  transfers between devices with their start and end apart: 3, of which 0 were waited for; matrix products, arithmetic and copies ran while one was open for 16% of the time, Pallas kernels for 8%

profile of v2, /device:TPU:0, one launch (start us, length us, event | category | flops | bytes accessed | tf_op | source)
XLA Modules:
  0.0 146.0 jit_solution(11208864872177159627)
XLA Ops:
  0.6 1.1 fusion.34
  1.7 0.8 fusion.35
  2.6 0.7 copy.128.refs_1_
  3.3 0.6 copy.127.refs_0_
  3.9 0.6 copy.129.refs_2_
  4.5 24.5 %shard_map.95 = (bf16[2,3,6,512]{3,2,1,0:T(8,128)(2,1)}, bf16[2,9,6,512]{3,2,1,0:T(8,128)(2,1)}, bf16[2,3,6,512]{3,2,1,0:T(8,128)(2,1)}, bf16[512,1536]{1,0:T(8,128)(2,1)}, bf16[512,512]{1,0:T(8,128)(2,1)}) custom-call(bf16[2,3,6,512]{3,2,1,0:T(8,128)(2,1)} %copy.127.refs_0_, bf16[2,9,6,512]{3,2,1,0:T(8,128)(2,1)} %copy.128.refs_1_, ...), custom_call_target="tpu_custom_call" | custom-call | tf_op jit(solution)/shard_map/pallas_call | solution.py:346
  29.1 0.4 collective-permute-start.2
  29.5 0.5 collective-permute-start
  30.0 1.2 fusion.30
  31.3 1.3 multiply_reduce_fusion
  32.6 1.1 maximum_convert_fusion
  33.9 2.1 %convolution_convert_fusion = bf16[288,1536]{1,0:T(8,128)(2,1)S(1)} fusion(bf16[512,1536]{1,0:T(8,128)(2,1)} %get-tuple-element.16, f32[288,512]{1,0:T(8,128)S(1)} %reshape.175, f32[288]{0:T(512)S(1)} %rsqrt.34, f32[288]{0:T(512)S(1)} %div.39), kind=kOutput, calls=%fused_computation.1 | convolution fusion | flops 453869568 | bytes 3049728 | tf_op jit(solution)/shard_map/dot_general | solution.py:403
  36.0 1.1 reshape.167
  37.1 0.3 copy.90
  37.4 0.3 fusion.31
  37.7 0.4 copy.111
  38.1 0.4 copy.112
  38.8 0.4 copy.110
  39.2 2.4 %fusion.36 = (f32[2,8,144]{2,1,0:T(8,128)S(1)}, f32[2,8,144,144]{2,3,1,0:T(8,128)}) fusion(pred[2,144,144]{1,2,0:T(8,128)(4,1)S(1)} %broadcast_compare_fusion, bf16[2,144,1,8,64]{1,4,3,0,2:T(8,128)(2,1)S(1)} %copy.112, bf16[2,144,1,8,64]{1,4,3,0,2:T(8,128)(2,1)S(1)} %copy.111), kind=kOutput, calls=%fused_computation.62 | convolution fusion | flops 43794576 | bytes 1967616 | tf_op jit(solution)/shard_map/sub | solution.py:423
  41.6 2.0 %fusion.2 = bf16[2,144,8,64]{1,3,2,0:T(8,128)(2,1)S(1)} fusion(f32[2,8,144,144]{2,3,1,0:T(8,128)} %get-tuple-element.48, f32[2,8,144]{2,1,0:T(8,128)S(1)} %get-tuple-element.47, bf16[2,144,1,8,64]{1,4,3,0,2:T(8,128)(2,1)S(1)} %copy.110), kind=kOutput, calls=%fused_computation.7 | convolution fusion | flops 43278336 | bytes 1926144 | tf_op jit(solution)/shard_map/whqk,wkhd->wqhd/dot_general | solution.py:425
  43.7 0.5 copy.95
  44.2 0.3 reshape.169
  44.7 0.3 convolution_convert_fusion.2
  45.1 0.7 fusion.33
  45.8 0.6 fusion.32
  46.4 12.2 %shard_map.96 = (bf16[2,3,6,512]{3,2,1,0:T(8,128)(2,1)}, bf16[2,9,6,512]{3,2,1,0:T(8,128)(2,1)}, bf16[2,3,6,512]{3,2,1,0:T(8,128)(2,1)}) custom-call(bf16[2,3,6,512]{3,2,1,0:T(8,128)(2,1)} %get-tuple-element.36.refs_0_, bf16[2,9,6,512]{3,2,1,0:T(8,128)(2,1)} %get-tuple-element.37.refs_1_, bf16[2,3,6,512]{3,2,1,0:T(8,128)(2,1)} %get-tuple-element.35.refs_2_), custom_call_target="tpu_custom_call" | custom-call | tf_op jit(solution)/shard_map/pallas_call | solution.py:346
  58.6 1.1 convert_add_fusion
  59.7 0.5 copy.107
  60.2 0.2 reduce_sum.66
  60.5 0.5 multiply_reduce_fusion.1
  60.9 0.3 copy.98
  61.2 0.1 copy.99
  61.6 0.5 reshape.173
  62.4 0.3 convolution_convert_fusion.3
  62.7 1.5 %convolution_convert_fusion.5 = bf16[72,256]{1,0:T(8,128)(2,1)S(1)} fusion(bf16[72,2048]{1,0:T(8,128)(2,1)S(1)} %multiply_convert_fusion, bf16[2048,256]{1,0:T(8,128)(2,1)} %collective-permute-done), kind=kOutput, calls=%fused_computation.14 | convolution fusion | flops 75515904 | bytes 1380352 | tf_op jit(solution)/shard_map/dot_general | solution.py:448
  64.3 1.5 %convolution_convert_fusion.4 = bf16[72,256]{1,0:T(8,128)(2,1)S(1)} fusion(bf16[72,2048]{1,0:T(8,128)(2,1)S(1)} %multiply_convert_fusion, bf16[2048,256]{1,0:T(8,128)(2,1)} %collective-permute-done.2), kind=kOutput, calls=%fused_computation.13 | convolution fusion | flops 75515904 | bytes 1380352 | tf_op jit(solution)/shard_map/dot_general | solution.py:448
  65.8 0.3 broadcast_select_fusion.7
  66.2 0.2 reshape.178
  66.4 0.2 fusion.29
  66.6 0.3 multiply_reduce_fusion.2
  67.1 0.2 reshape.174
  67.4 0.9 fusion.14.blocks_ref
  68.2 75.1 %shard_map.97 = bf16[8,18,512]{2,1,0:T(8,128)(2,1)} custom-call(bf16[8,18,512]{2,1,0:T(8,128)(2,1)} %fusion.14.blocks_ref, bf16[512,2048]{1,0:T(8,128)(2,1)} %two_hbm.1, bf16[2048,1024]{1,0:T(8,128)(2,1)} %in_hbm.1, bf16[1024,2048]{1,0:T(8,128)(2,1)} %out_hbm.1, bf16[2048,512]{1,0:T(8,128)(2,1)} %split_hbm.1), custom_call_target="tpu_custom_call" | custom-call | tf_op jit(solution)/shard_map/pallas_call | solution.py:199
  143.3 1.0 convert_bitcast_fusion
  144.3 0.2 copy.104
  144.5 0.2 reshape.179
  144.7 0.2 copy.105
  145.1 0.9 copy.108
  (39 shorter events, 1.7 us)
Async XLA Ops:
  29.1 35.2 %collective-permute-start.2 = (bf16[2048,256]{1,0:T(8,128)(2,1)}, bf16[2048,256]{1,0:T(8,128)(2,1)}, u32[]{:S(2)}, u32[]{:S(2)}) collective-permute-start(bf16[2048,256]{1,0:T(8,128)(2,1)} %param.11), channel_id=1, source_target_pairs={{0,8},{8,0},{16,24},{24,16},{1,9},{9,1},{17,25},{25,17},{2,10},{10... | collective-permute-start | bytes 3145736 | tf_op jit(solution)/shard_map/ppermute | solution.py:363
  29.5 32.7 %collective-permute-start = (bf16[2048,256]{1,0:T(8,128)(2,1)}, bf16[2048,256]{1,0:T(8,128)(2,1)}, u32[]{:S(2)}, u32[]{:S(2)}) collective-permute-start(bf16[2048,256]{1,0:T(8,128)(2,1)} %param.11), channel_id=1, source_target_pairs={{0,16},{8,24},{16,0},{24,8},{1,17},{9,25},{17,1},{25,9},{2,18},{10... | collective-permute-start | bytes 3145736 | tf_op jit(solution)/shard_map/ppermute | solution.py:363
  43.6 1.0 copy-start.3
  44.2 14.5 %copy-start.1 = (bf16[2,12,12,512]{3,0,2,1:T(2,128)(2,1)S(1)}, bf16[2,12,12,512]{3,0,2,1:T(2,128)(2,1)}, u32[]{:S(2)}) copy-start(bf16[2,12,12,512]{3,0,2,1:T(2,128)(2,1)} %param.8) | copy-start | bytes 884740
  60.2 2.5 %copy-start = (f32[2,12,12,512]{3,0,2,1:T(2,128)}, f32[2,12,12,512]{3,0,2,1:T(2,128)S(1)}, u32[]{:S(2)}) copy-start(f32[2,12,12,512]{3,0,2,1:T(2,128)S(1)} %copy.107) | copy-start | bytes 1769476
  60.2 2.2 %copy-start.2 = (bf16[2048,256]{1,0:T(8,128)(2,1)S(1)}, bf16[2048,256]{1,0:T(8,128)(2,1)}, u32[]{:S(2)}) copy-start(bf16[2048,256]{1,0:T(8,128)(2,1)} %param.11) | copy-start | bytes 3145732
  62.2 3.6 %collective-permute-start.1 = (bf16[2048,256]{1,0:T(8,128)(2,1)}, bf16[2048,256]{1,0:T(8,128)(2,1)S(1)}, u32[]{:S(2)}, u32[]{:S(2)}) collective-permute-start(bf16[2048,256]{1,0:T(8,128)(2,1)} %collective-permute-done), channel_id=1, source_target_pairs={{0,8},{8,0},{16,24},{24,16},{1,9},{9,1},{17,25},{25,17},{2,10},{10... | collective-permute-start | bytes 3145736 | tf_op jit(solution)/shard_map/ppermute | solution.py:363

commit v3 on v2

--- a/solution.py
+++ b/solution.py
@@ -31,9 +31,9 @@
 
 def coarse_kernel(
     blocks_ref, two_hbm, in_hbm, out_hbm, split_hbm, pieces_ref,
-    two, w_in, w_out, split, landed, features, sent, summed, own, gathered, normed, act,
-    sent2, summed2, gathered2, cols, sent3, landed3,
-    load_sem, send_sem, recv_sem,
+    two, w_in, w_out, split, landed, features, own, gathered, normed, act,
+    gathered2, cols, sent3, landed3, total, partial_sent, partial_came,
+    load_sem, send_sem, recv_sem, sum_send, sum_recv, relay_send, relay_recv,
 ):
     count = lax.axis_size("lon")
     me = lax.axis_index("lon")
@@ -92,33 +92,114 @@
 
         lax.fori_loop(1, count, body, 0)
 
-    def scatter_products(phase, left, weight, send, target):
+    chips = count // 2
+    z, y = me // 2, lax.rem(me, 2)
+    partner = me + 1 - 2 * y
+    up, down, over = 0, 1, 2
+
+    def hop(source, target, sent_sem, came_sem, peer):
+        return pltpu.make_async_remote_copy(
+            src_ref=source,
+            dst_ref=target,
+            send_sem=sent_sem,
+            recv_sem=came_sem,
+            device_id={"lon": peer},
+            device_id_type=pl.DeviceIdType.MESH,
+        )
+
+    def sum_hop(phase, kind, row, peer):
+        return hop(
+            partial_sent.at[phase, kind, row],
+            partial_came.at[phase, kind, row],
+            sum_send.at[phase, kind, row],
+            sum_recv.at[phase, kind, row],
+            peer,
+        )
+
+    def scatter_products(phase, left, weight):
         def product(peer):
             cut = pl.ds(pl.multiple_of(peer * width, width), width)
             return jnp.dot(left[...], weight[:, cut], preferred_element_type=jnp.float32)
 
-        def body(step, carry):
-            peer = lax.rem(me + step, count)
-            send[peer] = product(peer).astype(jnp.bfloat16)
-            copy_to(phase, peer, send.at[peer], target).start()
-            return carry
-
-        lax.fori_loop(1, count, body, 0)
-        total = product(me)
-        wait_from(phase, target)
-
-        def add(step, total):
-            return total + target[lax.rem(me + step, count)].astype(jnp.float32)
-
-        return lax.fori_loop(1, count, add, total)
+        def across(row):
+            partial_sent[phase, over, row] = product(2 * row + 1 - y).astype(jnp.bfloat16)
+            sum_hop(phase, over, row, partner).start()
+
+        def add(kind, row, peer):
+            sum_hop(phase, kind, row, peer).wait_recv()
+            total[...] += partial_came[phase, kind, row].astype(jnp.float32)
+
+        def onward(kind, row, behind, source, peer):
+            total[...] = product(2 * row + y)
+            add(over, row, partner)
+
+            @pl.when(behind)
+            def _():
+                add(kind, row, source)
+
+            partial_sent[phase, kind, row] = total[...].astype(jnp.bfloat16)
+            sum_hop(phase, kind, row, peer).start()
+
+        for far in range(chips - 1, 0, -1):
+            pl.when(z + far < chips)(lambda: across(z + far))
+            pl.when(z - far >= 0)(lambda: across(z - far))
+        across(z)
+        for far in range(chips - 1, 0, -1):
+            pl.when(z + far < chips)(lambda: onward(up, z + far, z > 0, me - 2, me + 2))
+            pl.when(z - far >= 0)(lambda: onward(down, z - far, z < chips - 1, me + 2, me - 2))
+        total[...] = product(me)
+        add(over, z, partner)
+        pl.when(z > 0)(lambda: add(up, z, me - 2))
+        pl.when(z < chips - 1)(lambda: add(down, z, me + 2))
+        return total[...]
+
+    def wait_products(phase):
+        for row in range(chips):
+            sum_hop(phase, over, row, partner).wait_send()
+        for far in range(1, chips):
+            pl.when(z + far < chips)(lambda: sum_hop(phase, up, z + far, me + 2).wait_send())
+            pl.when(z - far >= 0)(lambda: sum_hop(phase, down, z - far, me - 2).wait_send())
+
+    def relay(phase, target, kind, block, peer):
+        return hop(
+            target.at[block],
+            target.at[block],
+            relay_send.at[phase, kind, block],
+            relay_recv.at[phase, block],
+            peer,
+        )
+
+    def relays(phase, target, act_on, arriving):
+        pl.when(z < chips - 1)(lambda: act_on(relay(phase, target, up, me, me + 2)))
+        pl.when(z > 0)(lambda: act_on(relay(phase, target, down, me, me - 2)))
+        act_on(relay(phase, target, over, me, partner))
+        for far in range(1, chips):
+
+            @pl.when(z - far >= 0)
+            def _():
+                block = me - 2 * far
+                if arriving:
+                    relay(phase, target, up, block, me - 2).wait_recv()
+                pl.when(z < chips - 1)(
+                    lambda: act_on(relay(phase, target, up, block, me + 2))
+                )
+                act_on(relay(phase, target, over, block, partner))
+
+            @pl.when(z + far < chips)
+            def _():
+                block = me + 2 * far
+                if arriving:
+                    relay(phase, target, down, block, me + 2).wait_recv()
+                pl.when(z > 0)(lambda: act_on(relay(phase, target, down, block, me - 2)))
+                act_on(relay(phase, target, over, block, partner))
 
     def gather(phase, target):
-        def body(step, carry):
-            copy_to(phase, lax.rem(me + step, count), target.at[me], target).start()
-            return carry
-
-        lax.fori_loop(1, count, body, 0)
-        wait_from(phase, target)
+        relays(phase, target, lambda copy: copy.start(), True)
+        for row in range(chips):
+            relay(phase, target, over, 2 * row + 1 - y, partner).wait_recv()
+
+    def wait_gather(phase, target):
+        relays(phase, target, lambda copy: copy.wait_send(), False)
 
     def first(step, carry):
         peer = lax.rem(me + step, count)
@@ -132,10 +213,10 @@
         features[index * own_count : (index + 1) * own_count] = landed[index].astype(jnp.float32)
     normed[:, : features.shape[1]] = features[...].astype(jnp.bfloat16)
     loads[0].wait()
-    merged = scatter_products(1, normed.at[:, : features.shape[1]], two, sent, summed)
+    merged = scatter_products(0, normed.at[:, : features.shape[1]], two)
     own[...] = merged
     gathered[me] = merged.astype(jnp.bfloat16)
-    gather(2, gathered)
+    gather(0, gathered)
 
     total_width = count * width
     centre = gathered[0].astype(jnp.float32).sum(axis=-1, keepdims=True)
@@ -162,9 +243,9 @@
 
     lax.fori_loop(0, act.shape[1] // tile, hidden, 0)
     loads[2].wait()
-    mlp = scatter_products(3, act, w_out, sent2, summed2)
+    mlp = scatter_products(1, act, w_out)
     gathered2[me] = (own[...] + mlp).astype(jnp.bfloat16)
-    gather(4, gathered2)
+    gather(1, gathered2)
     for index in range(count):
         normed[:, index * width : (index + 1) * width] = gathered2[index]
     loads[3].wait()
@@ -174,19 +255,18 @@
 
     def last(step, carry):
         peer = lax.rem(me + step, count)
-        copy_to(5, peer, sent3.at[peer], landed3).start()
+        copy_to(1, peer, sent3.at[peer], landed3).start()
         return carry
 
     lax.fori_loop(1, count, last, 0)
     landed3[me] = sent3[me]
-    wait_from(5, landed3)
+    wait_from(1, landed3)
     pieces_ref[...] = landed3[...]
     wait_sent(0, lambda peer: blocks_ref.at[peer], landed)
-    wait_sent(1, lambda peer: sent.at[peer], summed)
-    wait_sent(2, lambda peer: gathered.at[me], gathered)
-    wait_sent(3, lambda peer: sent2.at[peer], summed2)
-    wait_sent(4, lambda peer: gathered2.at[me], gathered2)
-    wait_sent(5, lambda peer: sent3.at[peer], landed3)
+    wait_sent(1, lambda peer: sent3.at[peer], landed3)
+    for phase, target in enumerate((gathered, gathered2)):
+        wait_products(phase)
+        wait_gather(phase, target)
 
 
 def coarse_in_one(blocks, merge_two, mlp_in, mlp_out, split_weight):
@@ -208,21 +288,24 @@
             pltpu.VMEM(split_weight.shape, low),
             pltpu.VMEM((count, own_count, depth), low),
             pltpu.VMEM((tokens, depth), jnp.float32),
-            pltpu.VMEM((count, tokens, width), low),
-            pltpu.VMEM((count, tokens, width), low),
             pltpu.VMEM((tokens, width), jnp.float32),
             pltpu.VMEM((count, tokens, width), low),
             pltpu.VMEM((tokens, top), low),
             pltpu.VMEM((tokens, hidden), low),
             pltpu.VMEM((count, tokens, width), low),
-            pltpu.VMEM((count, tokens, width), low),
-            pltpu.VMEM((count, tokens, width), low),
             pltpu.VMEM((tokens, split_width), jnp.float32),
             pltpu.VMEM((count, own_count, split_width), low),
             pltpu.VMEM((count, own_count, split_width), low),
+            pltpu.VMEM((tokens, width), jnp.float32),
+            pltpu.VMEM((2, 3, count // 2, tokens, width), low),
+            pltpu.VMEM((2, 3, count // 2, tokens, width), low),
             pltpu.SemaphoreType.DMA((4,)),
-            pltpu.SemaphoreType.DMA((6, count)),
-            pltpu.SemaphoreType.DMA((6, count)),
+            pltpu.SemaphoreType.DMA((2, count)),
+            pltpu.SemaphoreType.DMA((2, count)),
+            pltpu.SemaphoreType.DMA((2, 3, count // 2)),
+            pltpu.SemaphoreType.DMA((2, 3, count // 2)),
+            pltpu.SemaphoreType.DMA((2, 3, count)),
+            pltpu.SemaphoreType.DMA((2, count)),
         ],
         compiler_params=pltpu.CompilerParams(
             collective_id=0, has_side_effects=True, vmem_limit_bytes=60 * 1024 * 1024
@@ -456,7 +539,7 @@
     merged1 = merged1.reshape(levels, rows // 2, cols // 2, MID)
     normed2 = layer_norm(cat_four(merged1.astype(jnp.float32))).astype(jnp.bfloat16)
     count = lax.axis_size("lon")
-    if merge_two.shape[1] % (count * 128) == 0:
+    if count % 2 == 0 and merge_two.shape[1] % (count * 128) == 0:
         blocks = normed2.reshape(normed2.shape[0], count, -1).transpose(1, 0, 2)
         pieces = coarse_in_one(blocks, merge_two, mlp_in, mlp_out, split_weight)
         pieces = pieces.transpose(1, 0, 2)

time: 147 us -> 148 us (level)
  Pallas kernels: 112 us -> 114 us
    pallas_call x1, Pallas kernels: 75.1 us -> 76.8 us  [coarse_in_one(): pl.pallas_call(coarse_kernel, out_shape=jax.ShapeDtypeStruct((count, own_...]
where the time goes in v3:
time: 148 us
  Pallas kernels  114 us (77%)
  local copies, waits for them, and re-layouts  13.5 us (9%)
  matrix products  10.5 us (7%)
  other arithmetic  8.07 us (5%)
    pallas_call x1, Pallas kernels, coarse_in_one(): pl.pallas_call(coarse_kernel, out_shape=jax.ShapeDtypeStruct((count, own_...  76.8 us
    pallas_call x2, Pallas kernels, exchange(): pl.pallas_call(functools.partial(halo_kernel, direction, shards), out_sha...  36.7 us
    unnamed x17, local copies, waits for them, and re-layouts  4.59 us
    dot_general x4, matrix products, on_device(): jnp.dot(normed1, part, preferred_element_type=jnp.float32)  3.69 us
  transfers between devices with their start and end apart: 3, of which 0 were waited for; matrix products, arithmetic and copies ran while one was open for 16% of the time, Pallas kernels for 8%

profile of v3, /device:TPU:0, one launch (start us, length us, event | category | flops | bytes accessed | tf_op | source)
XLA Modules:
  0.0 147.7 jit_solution(10941894142400245071)
XLA Ops:
  0.6 1.1 fusion.34
  1.7 0.8 fusion.35
  2.6 0.7 copy.128.refs_1_
  3.3 0.6 copy.127.refs_0_
  3.9 0.6 copy.129.refs_2_
  4.5 24.5 %shard_map.95 = (bf16[2,3,6,512]{3,2,1,0:T(8,128)(2,1)}, bf16[2,9,6,512]{3,2,1,0:T(8,128)(2,1)}, bf16[2,3,6,512]{3,2,1,0:T(8,128)(2,1)}, bf16[512,1536]{1,0:T(8,128)(2,1)}, bf16[512,512]{1,0:T(8,128)(2,1)}) custom-call(bf16[2,3,6,512]{3,2,1,0:T(8,128)(2,1)} %copy.127.refs_0_, bf16[2,9,6,512]{3,2,1,0:T(8,128)(2,1)} %copy.128.refs_1_, ...), custom_call_target="tpu_custom_call" | custom-call | tf_op jit(solution)/shard_map/pallas_call | solution.py:429
  29.1 0.4 collective-permute-start.2
  29.5 0.5 collective-permute-start
  30.0 1.2 fusion.30
  31.3 1.3 multiply_reduce_fusion
  32.6 1.1 maximum_convert_fusion
  33.9 2.1 %convolution_convert_fusion = bf16[288,1536]{1,0:T(8,128)(2,1)S(1)} fusion(bf16[512,1536]{1,0:T(8,128)(2,1)} %get-tuple-element.16, f32[288,512]{1,0:T(8,128)S(1)} %reshape.175, f32[288]{0:T(512)S(1)} %rsqrt.34, f32[288]{0:T(512)S(1)} %div.39), kind=kOutput, calls=%fused_computation.1 | convolution fusion | flops 453869568 | bytes 3049728 | tf_op jit(solution)/shard_map/dot_general | solution.py:486
  36.0 1.1 reshape.167
  37.1 0.3 copy.90
  37.4 0.3 fusion.31
  37.7 0.4 copy.111
  38.1 0.4 copy.112
  38.8 0.4 copy.110
  39.2 2.4 %fusion.36 = (f32[2,8,144]{2,1,0:T(8,128)S(1)}, f32[2,8,144,144]{2,3,1,0:T(8,128)}) fusion(pred[2,144,144]{1,2,0:T(8,128)(4,1)S(1)} %broadcast_compare_fusion, bf16[2,144,1,8,64]{1,4,3,0,2:T(8,128)(2,1)S(1)} %copy.112, bf16[2,144,1,8,64]{1,4,3,0,2:T(8,128)(2,1)S(1)} %copy.111), kind=kOutput, calls=%fused_computation.62 | convolution fusion | flops 43794576 | bytes 1967616 | tf_op jit(solution)/shard_map/sub | solution.py:506
  41.6 2.0 %fusion.2 = bf16[2,144,8,64]{1,3,2,0:T(8,128)(2,1)S(1)} fusion(f32[2,8,144,144]{2,3,1,0:T(8,128)} %get-tuple-element.48, f32[2,8,144]{2,1,0:T(8,128)S(1)} %get-tuple-element.47, bf16[2,144,1,8,64]{1,4,3,0,2:T(8,128)(2,1)S(1)} %copy.110), kind=kOutput, calls=%fused_computation.7 | convolution fusion | flops 43278336 | bytes 1926144 | tf_op jit(solution)/shard_map/whqk,wkhd->wqhd/dot_general | solution.py:508
  43.7 0.5 copy.95
  44.2 0.3 reshape.169
  44.7 0.3 convolution_convert_fusion.2
  45.1 0.7 fusion.33
  45.8 0.6 fusion.32
  46.4 12.2 %shard_map.96 = (bf16[2,3,6,512]{3,2,1,0:T(8,128)(2,1)}, bf16[2,9,6,512]{3,2,1,0:T(8,128)(2,1)}, bf16[2,3,6,512]{3,2,1,0:T(8,128)(2,1)}) custom-call(bf16[2,3,6,512]{3,2,1,0:T(8,128)(2,1)} %get-tuple-element.36.refs_0_, bf16[2,9,6,512]{3,2,1,0:T(8,128)(2,1)} %get-tuple-element.37.refs_1_, bf16[2,3,6,512]{3,2,1,0:T(8,128)(2,1)} %get-tuple-element.35.refs_2_), custom_call_target="tpu_custom_call" | custom-call | tf_op jit(solution)/shard_map/pallas_call | solution.py:429
  58.6 1.1 convert_add_fusion
  59.7 0.5 copy.107
  60.2 0.2 reduce_sum.66
  60.5 0.5 multiply_reduce_fusion.1
  60.9 0.3 copy.98
  61.2 0.1 copy.99
  61.6 0.5 reshape.173
  62.4 0.3 convolution_convert_fusion.3
  62.7 1.5 %convolution_convert_fusion.5 = bf16[72,256]{1,0:T(8,128)(2,1)S(1)} fusion(bf16[72,2048]{1,0:T(8,128)(2,1)S(1)} %multiply_convert_fusion, bf16[2048,256]{1,0:T(8,128)(2,1)} %collective-permute-done), kind=kOutput, calls=%fused_computation.14 | convolution fusion | flops 75515904 | bytes 1380352 | tf_op jit(solution)/shard_map/dot_general | solution.py:531
  64.3 1.5 %convolution_convert_fusion.4 = bf16[72,256]{1,0:T(8,128)(2,1)S(1)} fusion(bf16[72,2048]{1,0:T(8,128)(2,1)S(1)} %multiply_convert_fusion, bf16[2048,256]{1,0:T(8,128)(2,1)} %collective-permute-done.2), kind=kOutput, calls=%fused_computation.13 | convolution fusion | flops 75515904 | bytes 1380352 | tf_op jit(solution)/shard_map/dot_general | solution.py:531
  65.8 0.3 broadcast_select_fusion.7
  66.2 0.2 reshape.178
  66.4 0.2 fusion.29
  66.6 0.3 multiply_reduce_fusion.2
  67.1 0.2 reshape.174
  67.4 0.9 fusion.14.blocks_ref
  68.2 76.8 %shard_map.97 = bf16[8,18,512]{2,1,0:T(8,128)(2,1)} custom-call(bf16[8,18,512]{2,1,0:T(8,128)(2,1)} %fusion.14.blocks_ref, bf16[512,2048]{1,0:T(8,128)(2,1)} %two_hbm.1, bf16[2048,1024]{1,0:T(8,128)(2,1)} %in_hbm.1, bf16[1024,2048]{1,0:T(8,128)(2,1)} %out_hbm.1, bf16[2048,512]{1,0:T(8,128)(2,1)} %split_hbm.1), custom_call_target="tpu_custom_call" | custom-call | tf_op jit(solution)/shard_map/pallas_call | solution.py:279
  145.1 1.0 convert_bitcast_fusion
  146.0 0.2 copy.104
  146.2 0.2 reshape.179
  146.4 0.2 copy.105
  146.8 0.9 copy.108
  (39 shorter events, 1.7 us)
Async XLA Ops:
  29.1 35.2 %collective-permute-start.2 = (bf16[2048,256]{1,0:T(8,128)(2,1)}, bf16[2048,256]{1,0:T(8,128)(2,1)}, u32[]{:S(2)}, u32[]{:S(2)}) collective-permute-start(bf16[2048,256]{1,0:T(8,128)(2,1)} %param.11), channel_id=1, source_target_pairs={{0,8},{8,0},{16,24},{24,16},{1,9},{9,1},{17,25},{25,17},{2,10},{10... | collective-permute-start | bytes 3145736 | tf_op jit(solution)/shard_map/ppermute | solution.py:446
  29.5 32.7 %collective-permute-start = (bf16[2048,256]{1,0:T(8,128)(2,1)}, bf16[2048,256]{1,0:T(8,128)(2,1)}, u32[]{:S(2)}, u32[]{:S(2)}) collective-permute-start(bf16[2048,256]{1,0:T(8,128)(2,1)} %param.11), channel_id=1, source_target_pairs={{0,16},{8,24},{16,0},{24,8},{1,17},{9,25},{17,1},{25,9},{2,18},{10... | collective-permute-start | bytes 3145736 | tf_op jit(solution)/shard_map/ppermute | solution.py:446
  43.6 1.0 copy-start.3
  44.2 14.5 %copy-start.1 = (bf16[2,12,12,512]{3,0,2,1:T(2,128)(2,1)S(1)}, bf16[2,12,12,512]{3,0,2,1:T(2,128)(2,1)}, u32[]{:S(2)}) copy-start(bf16[2,12,12,512]{3,0,2,1:T(2,128)(2,1)} %param.8) | copy-start | bytes 884740
  60.2 2.6 %copy-start = (f32[2,12,12,512]{3,0,2,1:T(2,128)}, f32[2,12,12,512]{3,0,2,1:T(2,128)S(1)}, u32[]{:S(2)}) copy-start(f32[2,12,12,512]{3,0,2,1:T(2,128)S(1)} %copy.107) | copy-start | bytes 1769476
  60.2 2.2 %copy-start.2 = (bf16[2048,256]{1,0:T(8,128)(2,1)S(1)}, bf16[2048,256]{1,0:T(8,128)(2,1)}, u32[]{:S(2)}) copy-start(bf16[2048,256]{1,0:T(8,128)(2,1)} %param.11) | copy-start | bytes 3145732
  62.2 3.6 %collective-permute-start.1 = (bf16[2048,256]{1,0:T(8,128)(2,1)}, bf16[2048,256]{1,0:T(8,128)(2,1)S(1)}, u32[]{:S(2)}, u32[]{:S(2)}) collective-permute-start(bf16[2048,256]{1,0:T(8,128)(2,1)} %collective-permute-done), channel_id=1, source_target_pairs={{0,8},{8,0},{16,24},{24,16},{1,9},{9,1},{17,25},{25,17},{2,10},{10... | collective-permute-start | bytes 3145736 | tf_op jit(solution)/shard_map/ppermute | solution.py:446

commit v4 on v2

--- a/solution.py
+++ b/solution.py
@@ -270,9 +270,11 @@
 
     other_core = row + 1 - 2 * lax.rem(row, 2)
     other_chip = lax.rem(row + 2, 4)
+    side = lax.rem(col, 2)
+    pair = col + 1 - 2 * side
     partners = beside(1) + beside(-1)
     if shards:
-        partners += ((other_core, col), (other_chip, col))
+        partners += ((other_core, col), (other_chip, col), (row, pair))
     barrier = pltpu.get_barrier_semaphore()
     for partner in partners:
         pl.semaphore_signal(barrier, inc=1, device_id=partner, device_id_type=mesh)
@@ -297,40 +299,45 @@
         width = weights[index].shape[1]
         return wholes[index].at[:, pl.ds(pl.multiple_of(owner * width, width), width)]
 
-    relays = []
+    def half(ref, index, which):
+        depth = weights[index].shape[0] // 2
+        return ref.at[pl.ds(pl.multiple_of(which * depth, depth), depth)]
+
+    def send(index, kind, source, target, device):
+        copy = pltpu.make_async_remote_copy(
+            src_ref=source,
+            dst_ref=target,
+            send_sem=weight_send.at[index, kind],
+            recv_sem=weight_recv.at[index, kind],
+            device_id=device,
+            device_id_type=mesh,
+        )
+        copy.start()
+        return copy
+
+    moves = []
     for index in range(shards):
-        across = []
-        for kind, target in enumerate((other_chip, other_core)):
-            across.append(
-                pltpu.make_async_remote_copy(
-                    src_ref=weights[index],
-                    dst_ref=columns(index, row),
-                    send_sem=weight_send.at[index, kind],
-                    recv_sem=weight_recv.at[index, kind],
-                    device_id=(target, col),
-                    device_id_type=mesh,
-                )
-            )
-        for copy in across:
-            copy.start()
-        pltpu.make_async_copy(weights[index], columns(index, row), own_sem.at[index]).start()
-        relays.append(across)
+        mine, held = weights[index], columns(index, row)
+        away = send(
+            index, 0, half(mine, index, side), half(held, index, side), (other_chip, col)
+        )
+        moves.append([away, send(index, 1, mine, held, (other_core, col))])
+        pltpu.make_async_copy(mine, held, own_sem.at[index]).start()
     for index in range(shards):
-        relays[index][0].wait_recv()
-        relay = pltpu.make_async_remote_copy(
-            src_ref=columns(index, other_chip),
-            dst_ref=columns(index, other_chip),
-            send_sem=weight_send.at[index, 2],
-            recv_sem=weight_recv.at[index, 2],
-            device_id=(other_core, col),
-            device_id_type=mesh,
-        )
-        relay.start()
-        relays[index].append(relay)
+        moves[index][0].wait_recv()
+        part = half(columns(index, other_chip), index, side)
+        moves[index].append(send(index, 2, part, part, (row, pair)))
+        moves[index].append(send(index, 3, part, part, (other_core, col)))
     for index in range(shards):
-        relays[index][0].wait_send()
-        relays[index][1].wait()
-        relays[index][2].wait()
+        moves[index][2].wait_recv()
+        part = half(columns(index, other_chip), index, 1 - side)
+        moves[index].append(send(index, 4, part, part, (other_core, col)))
+    for index in range(shards):
+        away, core, paired, first, second = moves[index]
+        for copy in (away, core, paired, first, second):
+            copy.wait_send()
+        for copy in (core, first, second):
+            copy.wait_recv()
         pltpu.make_async_copy(weights[index], columns(index, row), own_sem.at[index]).wait()
     for copy in copies:
         copy.wait()
@@ -352,8 +359,8 @@
             pltpu.SemaphoreType.DMA((3,)),
             pltpu.SemaphoreType.DMA((3,)),
             pltpu.SemaphoreType.DMA((max(shards, 1),)),
-            pltpu.SemaphoreType.DMA((max(shards, 1), 3)),
-            pltpu.SemaphoreType.DMA((max(shards, 1), 3)),
+            pltpu.SemaphoreType.DMA((max(shards, 1), 5)),
+            pltpu.SemaphoreType.DMA((max(shards, 1), 5)),
         ],
         compiler_params=pltpu.CompilerParams(collective_id=identity, has_side_effects=True),
     )(*edges, *weights)
@@ -385,7 +392,7 @@
         fine_tokens[:, SHIFT_R:, :SHIFT_C],
         fine_tokens[:, :SHIFT_R, :SHIFT_C],
     )
-    if lat_count == 4:
+    if lat_count == 4 and lax.axis_size("lon") % 2 == 0:
         row_came, col_came, both_came, full_qkv, full_proj = exchange(
             edges, -1, (qkv_weight, proj_weight), 1
         )
@@ -442,7 +449,7 @@
     back = jnp.concatenate([upper, lower], axis=1)
     fine_out = fine_tokens.astype(jnp.float32) + back.astype(jnp.float32)
     normed1 = layer_norm(cat_four(fine_out)).astype(jnp.bfloat16)
-    if lat_count == 4:
+    if lat_count == 4 and lax.axis_size("lon") % 2 == 0:
         merged1 = in_owner_order(
             [
                 jnp.dot(normed1, part, preferred_element_type=jnp.float32).astype(jnp.bfloat16)

time: 147 us -> 144 us (0.980)
  Pallas kernels: 112 us -> 108 us
    pallas_call x2, Pallas kernels: 36.7 us -> 34 us  [exchange(): pl.pallas_call(functools.partial(halo_kernel, direction, shards), out_sha...]
  transfers between devices with their start and end apart: 3 -> 3, of which waited for: 0 -> 0; matrix products, arithmetic and copies ran while one was open for 16% -> 16% of each run, Pallas kernels for 8% -> 9%
where the time goes in v4:
time: 144 us; the launch traced here: 143 us
  Pallas kernels  108 us (75%)
  local copies, waits for them, and re-layouts  13.5 us (9%)
  matrix products  10.5 us (7%)
  other arithmetic  8.07 us (6%)
  starting transfers between devices  1.82 us (1%)
    pallas_call x1, Pallas kernels, coarse_in_one(): pl.pallas_call(coarse_kernel, out_shape=jax.ShapeDtypeStruct((count, own_...  74 us
    pallas_call x2, Pallas kernels, exchange(): pl.pallas_call(functools.partial(halo_kernel, direction, shards), out_sha...  34 us
    unnamed x17, local copies, waits for them, and re-layouts  4.59 us
    dot_general x4, matrix products, on_device(): jnp.dot(normed1, part, preferred_element_type=jnp.float32)  3.69 us
  transfers between devices with their start and end apart: 3, of which 0 were waited for; matrix products, arithmetic and copies ran while one was open for 16% of the time, Pallas kernels for 9%

profile of v4, /device:TPU:0, one launch (start us, length us, event | category | flops | bytes accessed | tf_op | source)
XLA Modules:
  0.0 143.0 jit_solution(17726244914736012082)
XLA Ops:
  0.6 1.1 fusion.34
  1.7 0.8 fusion.35
  2.6 0.7 copy.128.refs_1_
  3.3 0.6 copy.127.refs_0_
  3.9 0.6 copy.129.refs_2_
  4.5 21.6 %shard_map.95 = (bf16[2,3,6,512]{3,2,1,0:T(8,128)(2,1)}, bf16[2,9,6,512]{3,2,1,0:T(8,128)(2,1)}, bf16[2,3,6,512]{3,2,1,0:T(8,128)(2,1)}, bf16[512,1536]{1,0:T(8,128)(2,1)}, bf16[512,512]{1,0:T(8,128)(2,1)}) custom-call(bf16[2,3,6,512]{3,2,1,0:T(8,128)(2,1)} %copy.127.refs_0_, bf16[2,9,6,512]{3,2,1,0:T(8,128)(2,1)} %copy.128.refs_1_, ...), custom_call_target="tpu_custom_call" | custom-call | tf_op jit(solution)/shard_map/pallas_call | solution.py:353
  26.2 1.7 %collective-permute-start = (bf16[2048,256]{1,0:T(8,128)(2,1)}, bf16[2048,256]{1,0:T(8,128)(2,1)}, u32[]{:S(2)}, u32[]{:S(2)}) collective-permute-start(bf16[2048,256]{1,0:T(8,128)(2,1)} %param.11), channel_id=1, source_target_pairs={{0,16},{8,24},{16,0},{24,8},{1,17},{9,25},{17,1},{25,9},{2,18},{10... | collective-permute-start | bytes 3145736 | tf_op jit(solution)/shard_map/ppermute | solution.py:370
  27.9 1.2 fusion.30
  29.1 1.3 multiply_reduce_fusion
  30.5 1.1 maximum_convert_fusion
  31.8 2.1 %convolution_convert_fusion = bf16[288,1536]{1,0:T(8,128)(2,1)S(1)} fusion(bf16[512,1536]{1,0:T(8,128)(2,1)} %get-tuple-element.16, f32[288,512]{1,0:T(8,128)S(1)} %reshape.175, f32[288]{0:T(512)S(1)} %rsqrt.34, f32[288]{0:T(512)S(1)} %div.39), kind=kOutput, calls=%fused_computation.1 | convolution fusion | flops 453869568 | bytes 3049728 | tf_op jit(solution)/shard_map/dot_general | solution.py:410
  33.9 1.1 reshape.167
  35.0 0.3 copy.90
  35.3 0.3 fusion.31
  35.6 0.4 copy.111
  36.0 0.4 copy.112
  36.7 0.4 copy.110
  37.1 2.4 %fusion.36 = (f32[2,8,144]{2,1,0:T(8,128)S(1)}, f32[2,8,144,144]{2,3,1,0:T(8,128)}) fusion(pred[2,144,144]{1,2,0:T(8,128)(4,1)S(1)} %broadcast_compare_fusion, bf16[2,144,1,8,64]{1,4,3,0,2:T(8,128)(2,1)S(1)} %copy.112, bf16[2,144,1,8,64]{1,4,3,0,2:T(8,128)(2,1)S(1)} %copy.111), kind=kOutput, calls=%fused_computation.62 | convolution fusion | flops 43794576 | bytes 1967616 | tf_op jit(solution)/shard_map/sub | solution.py:430
  39.5 2.0 %fusion.2 = bf16[2,144,8,64]{1,3,2,0:T(8,128)(2,1)S(1)} fusion(f32[2,8,144,144]{2,3,1,0:T(8,128)} %get-tuple-element.48, f32[2,8,144]{2,1,0:T(8,128)S(1)} %get-tuple-element.47, bf16[2,144,1,8,64]{1,4,3,0,2:T(8,128)(2,1)S(1)} %copy.110), kind=kOutput, calls=%fused_computation.7 | convolution fusion | flops 43278336 | bytes 1926144 | tf_op jit(solution)/shard_map/whqk,wkhd->wqhd/dot_general | solution.py:432
  41.5 0.5 copy.95
  42.1 0.3 reshape.169
  42.6 0.3 convolution_convert_fusion.2
  43.0 0.7 fusion.33
  43.7 0.6 fusion.32
  44.3 12.4 %shard_map.96 = (bf16[2,3,6,512]{3,2,1,0:T(8,128)(2,1)}, bf16[2,9,6,512]{3,2,1,0:T(8,128)(2,1)}, bf16[2,3,6,512]{3,2,1,0:T(8,128)(2,1)}) custom-call(bf16[2,3,6,512]{3,2,1,0:T(8,128)(2,1)} %get-tuple-element.36.refs_0_, bf16[2,9,6,512]{3,2,1,0:T(8,128)(2,1)} %get-tuple-element.37.refs_1_, bf16[2,3,6,512]{3,2,1,0:T(8,128)(2,1)} %get-tuple-element.35.refs_2_), custom_call_target="tpu_custom_call" | custom-call | tf_op jit(solution)/shard_map/pallas_call | solution.py:353
  56.7 1.1 convert_add_fusion
  57.8 0.5 copy.107
  58.3 0.2 reduce_sum.66
  58.6 0.5 multiply_reduce_fusion.1
  59.0 0.3 copy.98
  59.3 0.1 copy.99
  59.5 0.1 copy.100
  59.7 0.5 reshape.173
  60.5 0.3 convolution_convert_fusion.3
  60.8 1.5 %convolution_convert_fusion.5 = bf16[72,256]{1,0:T(8,128)(2,1)S(1)} fusion(bf16[72,2048]{1,0:T(8,128)(2,1)S(1)} %multiply_convert_fusion, bf16[2048,256]{1,0:T(8,128)(2,1)} %collective-permute-done), kind=kOutput, calls=%fused_computation.14 | convolution fusion | flops 75515904 | bytes 1380352 | tf_op jit(solution)/shard_map/dot_general | solution.py:455
  62.4 1.5 %convolution_convert_fusion.4 = bf16[72,256]{1,0:T(8,128)(2,1)S(1)} fusion(bf16[72,2048]{1,0:T(8,128)(2,1)S(1)} %multiply_convert_fusion, bf16[2048,256]{1,0:T(8,128)(2,1)} %collective-permute-done.2), kind=kOutput, calls=%fused_computation.13 | convolution fusion | flops 75515904 | bytes 1380352 | tf_op jit(solution)/shard_map/dot_general | solution.py:455
  63.9 0.3 broadcast_select_fusion.7
  64.3 0.2 reshape.178
  64.5 0.2 fusion.29
  64.7 0.3 multiply_reduce_fusion.2
  65.2 0.2 reshape.174
  65.5 0.9 fusion.14.blocks_ref
  66.3 74.0 %shard_map.97 = bf16[8,18,512]{2,1,0:T(8,128)(2,1)} custom-call(bf16[8,18,512]{2,1,0:T(8,128)(2,1)} %fusion.14.blocks_ref, bf16[512,2048]{1,0:T(8,128)(2,1)} %two_hbm.1, bf16[2048,1024]{1,0:T(8,128)(2,1)} %in_hbm.1, bf16[1024,2048]{1,0:T(8,128)(2,1)} %out_hbm.1, bf16[2048,512]{1,0:T(8,128)(2,1)} %split_hbm.1), custom_call_target="tpu_custom_call" | custom-call | tf_op jit(solution)/shard_map/pallas_call | solution.py:199
  140.4 1.0 convert_bitcast_fusion
  141.3 0.2 copy.104
  141.5 0.2 reshape.179
  141.7 0.2 copy.105
  142.1 0.9 copy.108
  (39 shorter events, 1.7 us)
Async XLA Ops:
  26.2 36.2 %collective-permute-start.2 = (bf16[2048,256]{1,0:T(8,128)(2,1)}, bf16[2048,256]{1,0:T(8,128)(2,1)}, u32[]{:S(2)}, u32[]{:S(2)}) collective-permute-start(bf16[2048,256]{1,0:T(8,128)(2,1)} %param.11), channel_id=1, source_target_pairs={{0,8},{8,0},{16,24},{24,16},{1,9},{9,1},{17,25},{25,17},{2,10},{10... | collective-permute-start | bytes 3145736 | tf_op jit(solution)/shard_map/ppermute | solution.py:370
  26.2 34.1 %collective-permute-start = (bf16[2048,256]{1,0:T(8,128)(2,1)}, bf16[2048,256]{1,0:T(8,128)(2,1)}, u32[]{:S(2)}, u32[]{:S(2)}) collective-permute-start(bf16[2048,256]{1,0:T(8,128)(2,1)} %param.11), channel_id=1, source_target_pairs={{0,16},{8,24},{16,0},{24,8},{1,17},{9,25},{17,1},{25,9},{2,18},{10... | collective-permute-start | bytes 3145736 | tf_op jit(solution)/shard_map/ppermute | solution.py:370
  41.5 1.0 copy-start.3
  42.1 14.7 %copy-start.1 = (bf16[2,12,12,512]{3,0,2,1:T(2,128)(2,1)S(1)}, bf16[2,12,12,512]{3,0,2,1:T(2,128)(2,1)}, u32[]{:S(2)}) copy-start(bf16[2,12,12,512]{3,0,2,1:T(2,128)(2,1)} %param.8) | copy-start | bytes 884740
  58.3 2.5 %copy-start = (f32[2,12,12,512]{3,0,2,1:T(2,128)}, f32[2,12,12,512]{3,0,2,1:T(2,128)S(1)}, u32[]{:S(2)}) copy-start(f32[2,12,12,512]{3,0,2,1:T(2,128)S(1)} %copy.107) | copy-start | bytes 1769476
  58.3 2.2 %copy-start.2 = (bf16[2048,256]{1,0:T(8,128)(2,1)S(1)}, bf16[2048,256]{1,0:T(8,128)(2,1)}, u32[]{:S(2)}) copy-start(bf16[2048,256]{1,0:T(8,128)(2,1)} %param.11) | copy-start | bytes 3145732
  60.3 3.6 %collective-permute-start.1 = (bf16[2048,256]{1,0:T(8,128)(2,1)}, bf16[2048,256]{1,0:T(8,128)(2,1)S(1)}, u32[]{:S(2)}, u32[]{:S(2)}) collective-permute-start(bf16[2048,256]{1,0:T(8,128)(2,1)} %collective-permute-done), channel_id=1, source_target_pairs={{0,8},{8,0},{16,24},{24,16},{1,9},{9,1},{17,25},{25,17},{2,10},{10... | collective-permute-start | bytes 3145736 | tf_op jit(solution)/shard_map/ppermute | solution.py:370

commit v5 on v4

--- a/solution.py
+++ b/solution.py
@@ -33,7 +33,7 @@
     blocks_ref, two_hbm, in_hbm, out_hbm, split_hbm, pieces_ref,
     two, w_in, w_out, split, landed, features, sent, summed, own, gathered, normed, act,
     sent2, summed2, gathered2, cols, sent3, landed3,
-    load_sem, send_sem, recv_sem,
+    load_sem, send_sem, recv_sem, relay_send, relay_recv,
 ):
     count = lax.axis_size("lon")
     me = lax.axis_index("lon")
@@ -112,13 +112,61 @@
 
         return lax.fori_loop(1, count, add, total)
 
+    chips = count // 2
+    z, y = me // 2, lax.rem(me, 2)
+    partner = me + 1 - 2 * y
+    up, down, over = 0, 1, 2
+
+    def hop(source, target, sent_sem, came_sem, peer):
+        return pltpu.make_async_remote_copy(
+            src_ref=source,
+            dst_ref=target,
+            send_sem=sent_sem,
+            recv_sem=came_sem,
+            device_id={"lon": peer},
+            device_id_type=pl.DeviceIdType.MESH,
+        )
+
+    def relay(phase, target, kind, block, peer):
+        return hop(
+            target.at[block],
+            target.at[block],
+            relay_send.at[phase, kind, block],
+            relay_recv.at[phase, block],
+            peer,
+        )
+
+    def relays(phase, target, act_on, arriving):
+        pl.when(z < chips - 1)(lambda: act_on(relay(phase, target, up, me, me + 2)))
+        pl.when(z > 0)(lambda: act_on(relay(phase, target, down, me, me - 2)))
+        act_on(relay(phase, target, over, me, partner))
+        for far in range(1, chips):
+
+            @pl.when(z - far >= 0)
+            def _():
+                block = me - 2 * far
+                if arriving:
+                    relay(phase, target, up, block, me - 2).wait_recv()
+                pl.when(z < chips - 1)(
+                    lambda: act_on(relay(phase, target, up, block, me + 2))
+                )
+                act_on(relay(phase, target, over, block, partner))
+
+            @pl.when(z + far < chips)
+            def _():
+                block = me + 2 * far
+                if arriving:
+                    relay(phase, target, down, block, me + 2).wait_recv()
+                pl.when(z > 0)(lambda: act_on(relay(phase, target, down, block, me - 2)))
+                act_on(relay(phase, target, over, block, partner))
+
     def gather(phase, target):
-        def body(step, carry):
-            copy_to(phase, lax.rem(me + step, count), target.at[me], target).start()
-            return carry
-
-        lax.fori_loop(1, count, body, 0)
-        wait_from(phase, target)
+        relays(phase, target, lambda copy: copy.start(), True)
+        for row in range(chips):
+            relay(phase, target, over, 2 * row + 1 - y, partner).wait_recv()
+
+    def wait_gather(phase, target):
+        relays(phase, target, lambda copy: copy.wait_send(), False)
 
     def first(step, carry):
         peer = lax.rem(me + step, count)
@@ -135,7 +183,7 @@
     merged = scatter_products(1, normed.at[:, : features.shape[1]], two, sent, summed)
     own[...] = merged
     gathered[me] = merged.astype(jnp.bfloat16)
-    gather(2, gathered)
+    gather(0, gathered)
 
     total_width = count * width
     centre = gathered[0].astype(jnp.float32).sum(axis=-1, keepdims=True)
@@ -164,7 +212,7 @@
     loads[2].wait()
     mlp = scatter_products(3, act, w_out, sent2, summed2)
     gathered2[me] = (own[...] + mlp).astype(jnp.bfloat16)
-    gather(4, gathered2)
+    gather(1, gathered2)
     for index in range(count):
         normed[:, index * width : (index + 1) * width] = gathered2[index]
     loads[3].wait()
@@ -183,9 +231,9 @@
     pieces_ref[...] = landed3[...]
     wait_sent(0, lambda peer: blocks_ref.at[peer], landed)
     wait_sent(1, lambda peer: sent.at[peer], summed)
-    wait_sent(2, lambda peer: gathered.at[me], gathered)
+    wait_gather(0, gathered)
     wait_sent(3, lambda peer: sent2.at[peer], summed2)
-    wait_sent(4, lambda peer: gathered2.at[me], gathered2)
+    wait_gather(1, gathered2)
     wait_sent(5, lambda peer: sent3.at[peer], landed3)
 
 
@@ -223,6 +271,8 @@
             pltpu.SemaphoreType.DMA((4,)),
             pltpu.SemaphoreType.DMA((6, count)),
             pltpu.SemaphoreType.DMA((6, count)),
+            pltpu.SemaphoreType.DMA((2, 3, count)),
+            pltpu.SemaphoreType.DMA((2, count)),
         ],
         compiler_params=pltpu.CompilerParams(
             collective_id=0, has_side_effects=True, vmem_limit_bytes=60 * 1024 * 1024
@@ -463,7 +513,7 @@
     merged1 = merged1.reshape(levels, rows // 2, cols // 2, MID)
     normed2 = layer_norm(cat_four(merged1.astype(jnp.float32))).astype(jnp.bfloat16)
     count = lax.axis_size("lon")
-    if merge_two.shape[1] % (count * 128) == 0:
+    if count % 2 == 0 and merge_two.shape[1] % (count * 128) == 0:
         blocks = normed2.reshape(normed2.shape[0], count, -1).transpose(1, 0, 2)
         pieces = coarse_in_one(blocks, merge_two, mlp_in, mlp_out, split_weight)
         pieces = pieces.transpose(1, 0, 2)

time: 144 us -> 143 us (level); the launches traced: 143 us -> 140 us
  Pallas kernels: 108 us -> 105 us
    pallas_call x1, Pallas kernels: 74 us -> 71.1 us  [coarse_in_one(): pl.pallas_call(coarse_kernel, out_shape=jax.ShapeDtypeStruct((count, own_...]
  transfers between devices with their start and end apart: 3 -> 3, of which waited for: 0 -> 0; matrix products, arithmetic and copies ran while one was open for 16% -> 17% of each run, Pallas kernels for 9% -> 9%
where the time goes in v5:
time: 143 us; the launch traced here: 140 us
  Pallas kernels  105 us (73%)
  local copies, waits for them, and re-layouts  13.5 us (9%)
  matrix products  10.5 us (7%)
  other arithmetic  8.07 us (6%)
  starting transfers between devices  1.82 us (1%)
    pallas_call x1, Pallas kernels, coarse_in_one(): pl.pallas_call(coarse_kernel, out_shape=jax.ShapeDtypeStruct((count, own_...  71.1 us
    pallas_call x2, Pallas kernels, exchange(): pl.pallas_call(functools.partial(halo_kernel, direction, shards), out_sha...  34 us
    unnamed x17, local copies, waits for them, and re-layouts  4.59 us
    dot_general x4, matrix products, on_device(): jnp.dot(normed1, part, preferred_element_type=jnp.float32)  3.68 us
  transfers between devices with their start and end apart: 3, of which 0 were waited for; matrix products, arithmetic and copies ran while one was open for 17% of the time, Pallas kernels for 9%

profile of v5, /device:TPU:0, one launch (start us, length us, event | category | flops | bytes accessed | tf_op | source)
XLA Modules:
  0.0 140.1 jit_solution(17087167868390770992)
XLA Ops:
  0.6 1.1 fusion.34
  1.7 0.8 fusion.35
  2.6 0.7 copy.128.refs_1_
  3.3 0.6 copy.127.refs_0_
  3.9 0.6 copy.129.refs_2_
  4.5 21.6 %shard_map.95 = (bf16[2,3,6,512]{3,2,1,0:T(8,128)(2,1)}, bf16[2,9,6,512]{3,2,1,0:T(8,128)(2,1)}, bf16[2,3,6,512]{3,2,1,0:T(8,128)(2,1)}, bf16[512,1536]{1,0:T(8,128)(2,1)}, bf16[512,512]{1,0:T(8,128)(2,1)}) custom-call(bf16[2,3,6,512]{3,2,1,0:T(8,128)(2,1)} %copy.127.refs_0_, bf16[2,9,6,512]{3,2,1,0:T(8,128)(2,1)} %copy.128.refs_1_, ...), custom_call_target="tpu_custom_call" | custom-call | tf_op jit(solution)/shard_map/pallas_call | solution.py:403
  26.2 1.7 %collective-permute-start = (bf16[2048,256]{1,0:T(8,128)(2,1)}, bf16[2048,256]{1,0:T(8,128)(2,1)}, u32[]{:S(2)}, u32[]{:S(2)}) collective-permute-start(bf16[2048,256]{1,0:T(8,128)(2,1)} %param.11), channel_id=1, source_target_pairs={{0,16},{8,24},{16,0},{24,8},{1,17},{9,25},{17,1},{25,9},{2,18},{10... | collective-permute-start | bytes 3145736 | tf_op jit(solution)/shard_map/ppermute | solution.py:420
  27.9 1.2 fusion.30
  29.1 1.3 multiply_reduce_fusion
  30.5 1.1 maximum_convert_fusion
  31.8 2.1 %convolution_convert_fusion = bf16[288,1536]{1,0:T(8,128)(2,1)S(1)} fusion(bf16[512,1536]{1,0:T(8,128)(2,1)} %get-tuple-element.16, f32[288,512]{1,0:T(8,128)S(1)} %reshape.175, f32[288]{0:T(512)S(1)} %rsqrt.34, f32[288]{0:T(512)S(1)} %div.39), kind=kOutput, calls=%fused_computation.1 | convolution fusion | flops 453869568 | bytes 3049728 | tf_op jit(solution)/shard_map/dot_general | solution.py:460
  33.9 1.1 reshape.167
  35.0 0.3 copy.90
  35.3 0.3 fusion.31
  35.6 0.4 copy.111
  36.0 0.4 copy.112
  36.7 0.4 copy.110
  37.1 2.4 %fusion.36 = (f32[2,8,144]{2,1,0:T(8,128)S(1)}, f32[2,8,144,144]{2,3,1,0:T(8,128)}) fusion(pred[2,144,144]{1,2,0:T(8,128)(4,1)S(1)} %broadcast_compare_fusion, bf16[2,144,1,8,64]{1,4,3,0,2:T(8,128)(2,1)S(1)} %copy.112, bf16[2,144,1,8,64]{1,4,3,0,2:T(8,128)(2,1)S(1)} %copy.111), kind=kOutput, calls=%fused_computation.62 | convolution fusion | flops 43794576 | bytes 1967616 | tf_op jit(solution)/shard_map/sub | solution.py:480
  39.5 2.0 %fusion.2 = bf16[2,144,8,64]{1,3,2,0:T(8,128)(2,1)S(1)} fusion(f32[2,8,144,144]{2,3,1,0:T(8,128)} %get-tuple-element.48, f32[2,8,144]{2,1,0:T(8,128)S(1)} %get-tuple-element.47, bf16[2,144,1,8,64]{1,4,3,0,2:T(8,128)(2,1)S(1)} %copy.110), kind=kOutput, calls=%fused_computation.7 | convolution fusion | flops 43278336 | bytes 1926144 | tf_op jit(solution)/shard_map/whqk,wkhd->wqhd/dot_general | solution.py:482
  41.5 0.5 copy.95
  42.1 0.3 reshape.169
  42.6 0.3 convolution_convert_fusion.2
  43.0 0.7 fusion.33
  43.7 0.6 fusion.32
  44.3 12.4 %shard_map.96 = (bf16[2,3,6,512]{3,2,1,0:T(8,128)(2,1)}, bf16[2,9,6,512]{3,2,1,0:T(8,128)(2,1)}, bf16[2,3,6,512]{3,2,1,0:T(8,128)(2,1)}) custom-call(bf16[2,3,6,512]{3,2,1,0:T(8,128)(2,1)} %get-tuple-element.36.refs_0_, bf16[2,9,6,512]{3,2,1,0:T(8,128)(2,1)} %get-tuple-element.37.refs_1_, bf16[2,3,6,512]{3,2,1,0:T(8,128)(2,1)} %get-tuple-element.35.refs_2_), custom_call_target="tpu_custom_call" | custom-call | tf_op jit(solution)/shard_map/pallas_call | solution.py:403
  56.7 1.1 convert_add_fusion
  57.8 0.5 copy.107
  58.3 0.2 reduce_sum.66
  58.6 0.5 multiply_reduce_fusion.1
  59.0 0.3 copy.98
  59.3 0.1 copy.99
  59.5 0.1 copy.100
  59.7 0.5 reshape.173
  60.5 0.3 convolution_convert_fusion.3
  60.8 1.5 %convolution_convert_fusion.5 = bf16[72,256]{1,0:T(8,128)(2,1)S(1)} fusion(bf16[72,2048]{1,0:T(8,128)(2,1)S(1)} %multiply_convert_fusion, bf16[2048,256]{1,0:T(8,128)(2,1)} %collective-permute-done), kind=kOutput, calls=%fused_computation.14 | convolution fusion | flops 75515904 | bytes 1380352 | tf_op jit(solution)/shard_map/dot_general | solution.py:505
  62.4 1.5 %convolution_convert_fusion.4 = bf16[72,256]{1,0:T(8,128)(2,1)S(1)} fusion(bf16[72,2048]{1,0:T(8,128)(2,1)S(1)} %multiply_convert_fusion, bf16[2048,256]{1,0:T(8,128)(2,1)} %collective-permute-done.2), kind=kOutput, calls=%fused_computation.13 | convolution fusion | flops 75515904 | bytes 1380352 | tf_op jit(solution)/shard_map/dot_general | solution.py:505
  63.9 0.3 broadcast_select_fusion.7
  64.3 0.2 reshape.178
  64.5 0.2 fusion.29
  64.7 0.3 multiply_reduce_fusion.2
  65.2 0.2 reshape.174
  65.5 0.9 fusion.14.blocks_ref
  66.3 71.1 %shard_map.97 = bf16[8,18,512]{2,1,0:T(8,128)(2,1)} custom-call(bf16[8,18,512]{2,1,0:T(8,128)(2,1)} %fusion.14.blocks_ref, bf16[512,2048]{1,0:T(8,128)(2,1)} %two_hbm.1, bf16[2048,1024]{1,0:T(8,128)(2,1)} %in_hbm.1, bf16[1024,2048]{1,0:T(8,128)(2,1)} %out_hbm.1, bf16[2048,512]{1,0:T(8,128)(2,1)} %split_hbm.1), custom_call_target="tpu_custom_call" | custom-call | tf_op jit(solution)/shard_map/pallas_call | solution.py:247
  137.4 1.0 convert_bitcast_fusion
  138.4 0.2 copy.104
  138.6 0.2 reshape.179
  138.8 0.2 copy.105
  139.2 0.9 copy.108
  (39 shorter events, 1.7 us)
Async XLA Ops:
  26.2 36.2 %collective-permute-start.2 = (bf16[2048,256]{1,0:T(8,128)(2,1)}, bf16[2048,256]{1,0:T(8,128)(2,1)}, u32[]{:S(2)}, u32[]{:S(2)}) collective-permute-start(bf16[2048,256]{1,0:T(8,128)(2,1)} %param.11), channel_id=1, source_target_pairs={{0,8},{8,0},{16,24},{24,16},{1,9},{9,1},{17,25},{25,17},{2,10},{10... | collective-permute-start | bytes 3145736 | tf_op jit(solution)/shard_map/ppermute | solution.py:420
  26.2 34.1 %collective-permute-start = (bf16[2048,256]{1,0:T(8,128)(2,1)}, bf16[2048,256]{1,0:T(8,128)(2,1)}, u32[]{:S(2)}, u32[]{:S(2)}) collective-permute-start(bf16[2048,256]{1,0:T(8,128)(2,1)} %param.11), channel_id=1, source_target_pairs={{0,16},{8,24},{16,0},{24,8},{1,17},{9,25},{17,1},{25,9},{2,18},{10... | collective-permute-start | bytes 3145736 | tf_op jit(solution)/shard_map/ppermute | solution.py:420
  41.5 1.0 copy-start.3
  42.1 14.7 %copy-start.1 = (bf16[2,12,12,512]{3,0,2,1:T(2,128)(2,1)S(1)}, bf16[2,12,12,512]{3,0,2,1:T(2,128)(2,1)}, u32[]{:S(2)}) copy-start(bf16[2,12,12,512]{3,0,2,1:T(2,128)(2,1)} %param.8) | copy-start | bytes 884740
  58.3 2.5 %copy-start = (f32[2,12,12,512]{3,0,2,1:T(2,128)}, f32[2,12,12,512]{3,0,2,1:T(2,128)S(1)}, u32[]{:S(2)}) copy-start(f32[2,12,12,512]{3,0,2,1:T(2,128)S(1)} %copy.107) | copy-start | bytes 1769476
  58.3 2.2 %copy-start.2 = (bf16[2048,256]{1,0:T(8,128)(2,1)S(1)}, bf16[2048,256]{1,0:T(8,128)(2,1)}, u32[]{:S(2)}) copy-start(bf16[2048,256]{1,0:T(8,128)(2,1)} %param.11) | copy-start | bytes 3145732
  60.3 3.6 %collective-permute-start.1 = (bf16[2048,256]{1,0:T(8,128)(2,1)}, bf16[2048,256]{1,0:T(8,128)(2,1)S(1)}, u32[]{:S(2)}, u32[]{:S(2)}) collective-permute-start(bf16[2048,256]{1,0:T(8,128)(2,1)} %collective-permute-done), channel_id=1, source_target_pairs={{0,8},{8,0},{16,24},{24,16},{1,9},{9,1},{17,25},{25,17},{2,10},{10... | collective-permute-start | bytes 3145736 | tf_op jit(solution)/shard_map/ppermute | solution.py:420
